TPU v7x, 128 devices: a whole 4x4x4 slice. The times are simulated.
128 devices in a mesh: band: 4 (over y), expert: 32 (over z, x, core).
Axes of the slice: x: 4, y: 4, z: 4, core: 2. Of those that a mesh axis runs over, the one named last changes fastest.
Arguments:
- features: bfloat16 [32, 32, 64, 512], P('expert', None, 'band'), may hold values from -18 to 18
- routes: int32 [32, 4, 32, 16, 1], P('expert', 'band'), may hold values from 0 to 31; in each aligned block of 512 rows (0 to 511, 512 to 1023, ..., all dimensions but the last counted through in order) at most 32 rows name the same one
- qkv_regular: bfloat16 [512, 1536], replicated, may hold values from -0.25 to 0.25
- proj_regular: bfloat16 [512, 512], replicated, may hold values from -0.25 to 0.25
- table_regular: float32 [225, 16], replicated, may hold values from -4 to 4
- gain_regular: float32 [512], replicated, may hold values from 0.5 to 1.5
- mlp_up: bfloat16 [512, 2048], replicated, may hold values from -0.25 to 0.25
- mlp_down: bfloat16 [2048, 512], replicated, may hold values from -0.125 to 0.125
- gain_mlp: float32 [512], replicated, may hold values from 0.5 to 1.5
- qkv_shifted: bfloat16 [512, 1536], replicated, may hold values from -0.25 to 0.25
- proj_shifted: bfloat16 [512, 512], replicated, may hold values from -0.25 to 0.25
- table_shifted: float32 [225, 16], replicated, may hold values from -4 to 4
- gain_shifted: float32 [512], replicated, may hold values from 0.5 to 1.5
- expert_in: bfloat16 [32, 512, 2048], P('expert', None, 'band'), may hold values from -0.25 to 0.25
- expert_out: bfloat16 [32, 2048, 512], P('expert', 'band'), may hold values from -0.125 to 0.125
- gain_expert: float32 [512], replicated, may hold values from 0.5 to 1.5
Outputs:
- encoded: bfloat16 [32, 32, 64, 512], P('expert', None, 'band')
Inputs may be any that keep to these rules, and one draw needn't show every extreme that they name: `routes`: within one crop and one band (an aligned block of 512 tokens) no expert is named by more than 32 tokens, a bound that some block reaches.
All inputs are finite; a program needn't handle non-finite values.
Results may differ from a plain program's by a relative error of at most 0.015.
Values may be sent and summed in bfloat16 or wider, within the bound.
A program may use at most 128 MiB of HBM per device.

v0:
```python
import functools
import jax
import jax.numpy as jnp
from jax import lax
from jax.experimental import pallas as pl
from jax.experimental.pallas import tpu as pltpu
from jax.sharding import PartitionSpec as P

MESH = pl.DeviceIdType.MESH
F32 = jnp.float32
BF16 = jnp.bfloat16
WIN = 8
HALF = WIN // 2
CELLS = WIN * WIN
LANES = 128
LOG2E = 1.4426950408889634
ROOT_HALF = 0.7071067811865476


def dot(a, b):
    return jnp.dot(a, b, preferred_element_type=F32)


def dot_over(a, b, dim_a, dim_b):
    return lax.dot_general(a, b, (((dim_a,), (dim_b,)), ((), ())), preferred_element_type=F32)


def gelu(v):
    return (0.5 * v) * (1.0 + lax.erf(v * ROOT_HALF))


def layer_norm(values, gain_vec):
    centre = jnp.mean(values, axis=-1, keepdims=True)
    offsets = values - centre
    spread = jnp.mean(offsets * offsets, axis=-1, keepdims=True)
    return offsets * lax.rsqrt(spread + 1e-05) * gain_vec


def turn(tiles):
    return pltpu.roll(tiles, HALF, axis=tiles.ndim - 2)


def cell_is_low(shape):
    return lax.broadcasted_iota(jnp.int32, shape, len(shape) - 2) < HALF


def window_bias(flat_ref, first_head, bias_ref):
    pitch = 2 * WIN
    width = pitch * pitch
    even = lax.broadcasted_iota(jnp.int32, (WIN, LANES), 1) % pitch < WIN
    for group in range(4):
        for pair in range(2):
            head = first_head + group * 4 + pair * 2
            row_even = jnp.broadcast_to(flat_ref[head : head + 1, :], (WIN, width))
            row_odd = jnp.broadcast_to(flat_ref[head + 1 : head + 2, :], (WIN, width))
            for key_row in range(WIN):
                back = (WIN - 1 - key_row) * pitch + WIN - 1
                a = pltpu.roll(row_even, (width - back) % width, axis=1, stride=1, stride_axis=0)
                b = pltpu.roll(
                    row_odd, (width - back + WIN) % width, axis=1, stride=1, stride_axis=0
                )
                bias_ref[
                    group,
                    key_row * WIN : (key_row + 1) * WIN,
                    pair * LANES : (pair + 1) * LANES,
                ] = jnp.where(even, a[:, :LANES], b[:, :LANES])


def spread_heads(q):
    head = lax.broadcasted_iota(jnp.int32, (1, 1, LANES), 2) // 32
    tiles = q.astype(F32).reshape(WIN, WIN, LANES)
    pieces = []
    for pair in range(2):
        both = [jnp.where(head == pair * 2 + k, tiles, 0.0)[:, None] for k in range(2)]
        pieces.append(jnp.concatenate(both, axis=1).reshape(2 * CELLS, LANES))
    return jnp.concatenate(pieces, axis=0).astype(BF16)


def gather_heads(o):
    head = lax.broadcasted_iota(jnp.int32, (1, 1, LANES), 2) // 32
    parts = o.reshape(2, WIN, 2, WIN, LANES)
    low = jnp.where(head == 0, parts[0, :, 0], parts[0, :, 1])
    high = jnp.where(head == 2, parts[1, :, 0], parts[1, :, 1])
    return jnp.where(head < 2, low, high).reshape(CELLS, LANES)


def soften(s):
    e = jnp.exp2(s - jnp.max(s, axis=0, keepdims=True))
    return (e * (1.0 / jnp.sum(e, axis=0, keepdims=True))).astype(BF16)


def front_kernel(
    x_ref,
    flat_ref,
    gains_ref,
    qkv_r_hbm,
    proj_r_hbm,
    up_hbm,
    down_hbm,
    qkv_s_hbm,
    proj_s_hbm,
    out_ref,
    qkv_r,
    proj_r,
    up,
    down,
    qkv_s,
    proj_s,
    load_sem,
    bias_r,
    bias_s,
    tiles,
    qkv_buf,
    edge_buf,
    heads,
    to_left,
    to_right,
    from_left,
    from_right,
    send_sem,
    recv_sem,
):
    band = lax.axis_index("band")
    bands = lax.axis_size("band")
    right = lax.rem(band + 1, bands)
    left = lax.rem(band + bands - 1, bands)
    loads = [
        pltpu.make_async_copy(src, dst, load_sem.at[n])
        for n, (src, dst) in enumerate(
            (
                (qkv_r_hbm, qkv_r),
                (proj_r_hbm, proj_r),
                (up_hbm, up),
                (down_hbm, down),
                (qkv_s_hbm, qkv_s),
                (proj_s_hbm, proj_s),
            )
        )
    ]
    for load in loads:
        load.start()
    barrier = pltpu.get_barrier_semaphore()
    for other in (left, right):
        pl.semaphore_signal(barrier, inc=1, device_id={"band": other}, device_id_type=MESH)
    pl.semaphore_wait(barrier, 2)

    scale = LOG2E * 32**-0.5
    window_bias(flat_ref, 0, bias_r)
    window_bias(flat_ref, 16, bias_s)
    for load in loads[:4]:
        load.wait()

    def sends(part):
        return [
            pltpu.make_async_remote_copy(
                src_ref=to_left.at[part],
                dst_ref=from_right.at[part],
                send_sem=send_sem.at[0, part],
                recv_sem=recv_sem.at[0, part],
                device_id={"band": left},
                device_id_type=MESH,
            ),
            pltpu.make_async_remote_copy(
                src_ref=to_right.at[part],
                dst_ref=from_left.at[part],
                send_sem=send_sem.at[1, part],
                recv_sem=recv_sem.at[1, part],
                device_id={"band": right},
                device_id_type=MESH,
            ),
        ]

    low_cell = cell_is_low((1, WIN, 512))

    def first_part(part, carry):
        x3 = x_ref[0, pl.ds(part * 16, 16)].astype(F32)
        xf = jnp.concatenate(
            [
                x3[r * 8 : r * 8 + 8, c * 8 : c * 8 + 8, :].reshape(CELLS, 512)
                for r in range(2)
                for c in range(2)
            ],
            axis=0,
        )
        qkv_buf[...] = dot(xf.astype(BF16), qkv_r[...]).astype(BF16)
        for w in range(4):
            rows = slice(w * CELLS, (w + 1) * CELLS)
            for g in range(4):
                q = qkv_buf[rows, g * 128 : g * 128 + 128]
                k = qkv_buf[rows, 512 + g * 128 : 640 + g * 128]
                v = qkv_buf[rows, 1024 + g * 128 : 1152 + g * 128]
                s = dot_over(k, spread_heads(q), 1, 1) * scale + bias_r[g]
                heads[rows, g * 128 : g * 128 + 128] = gather_heads(
                    dot_over(soften(s), v, 0, 0)
                ).astype(BF16)
        first = (xf + layer_norm(dot(heads[...], proj_r[...]), gains_ref[0:1, :])).astype(BF16)
        total = jnp.zeros((256, 512), F32)
        for f in range(4):
            hidden = gelu(dot(first, up[:, f * 512 : f * 512 + 512])).astype(BF16)
            total = total + dot(hidden, down[f * 512 : f * 512 + 512, :])
        second = (first.astype(F32) + layer_norm(total, gains_ref[1:2, :])).astype(BF16).astype(F32)
        for r in range(2):
            rows = pl.ds(part * 16 + r * 8, 8)
            w0 = second[r * 128 : r * 128 + 64].reshape(WIN, WIN, 512)
            w1 = second[r * 128 + 64 : r * 128 + 128].reshape(WIN, WIN, 512)
            tiles[rows, 1] = w0
            tiles[rows, 2] = w1
            to_left[part, r * 32 : r * 32 + 32] = (
                jnp.where(low_cell, w0[:HALF], turn(w0[HALF:])).reshape(32, 512).astype(BF16)
            )
            to_right[part, r * 32 : r * 32 + 32] = (
                jnp.where(low_cell, turn(w1[HALF:]), w1[:HALF]).reshape(32, 512).astype(BF16)
            )
        for send in sends(part):
            send.start()
        return carry

    lax.fori_loop(0, 2, first_part, 0)

    def shifted(column):
        pieces = []
        for w in range(4):
            for start in (w * 8 + 4, (w * 8 + 8) % 32):
                a = tiles[start : start + 4, column]
                b = tiles[start : start + 4, column + 1]
                pieces.append(turn(jnp.where(low_cell, b, a)))
        return jnp.concatenate(pieces, axis=0)

    def finish(x, first_row):
        third = x + layer_norm(dot(heads[...], proj_s[...]), gains_ref[2:3, :])
        out_ref[first_row : first_row + 256, :] = third.astype(BF16)

    key = lax.broadcasted_iota(jnp.int32, (CELLS, 256), 0)
    lane = lax.broadcasted_iota(jnp.int32, (CELLS, 256), 1)
    low_j = lane % 8 < HALF
    row_apart = (key // 8 < HALF) != ((lane // 16) % 8 < HALF)
    col_apart = ((key % 8 < HALF) != low_j) & (
        (low_j & (band == bands - 1)) | (jnp.logical_not(low_j) & (band == 0))
    )
    mask_row = jnp.where(row_apart, -100.0 * LOG2E, 0.0)
    mask_col = jnp.where(col_apart, -100.0 * LOG2E, 0.0)
    mask_both = jnp.where(row_apart | col_apart, -100.0 * LOG2E, 0.0)

    for load in loads[4:]:
        load.wait()
    mid = shifted(1).reshape(256, 512)
    qkv_buf[...] = dot(mid.astype(BF16), qkv_s[...]).astype(BF16)
    for w in range(4):
        rows = slice(w * CELLS, (w + 1) * CELLS)
        for g in range(4):
            q = qkv_buf[rows, g * 128 : g * 128 + 128]
            k = qkv_buf[rows, 512 + g * 128 : 640 + g * 128]
            v = qkv_buf[rows, 1024 + g * 128 : 1152 + g * 128]
            s = dot_over(k, spread_heads(q), 1, 1) * scale + bias_s[g]
            if w == 3:
                s = s + mask_row
            heads[rows, g * 128 : g * 128 + 128] = gather_heads(
                dot_over(soften(s), v, 0, 0)
            ).astype(BF16)
    finish(mid, 0)

    for part in range(2):
        for send in sends(part):
            send.wait()
        for r in range(2):
            top = part * 16 + r * 8
            h = from_left[part, r * 32 : r * 32 + 32].astype(F32).reshape(HALF, WIN, 512)
            tiles[top : top + 4, 0] = h
            tiles[top + 4 : top + 8, 0] = turn(h)
            h = from_right[part, r * 32 : r * 32 + 32].astype(F32).reshape(HALF, WIN, 512)
            tiles[top : top + 4, 3] = h
            tiles[top + 4 : top + 8, 3] = turn(h)
    edge0 = shifted(0)
    edge2 = shifted(2)
    edge = jnp.where(low_cell, edge2, edge0).reshape(256, 512)
    qkv_buf[:, :512] = dot(edge.astype(BF16), qkv_s[:, :512]).astype(BF16)
    qkv_buf[:, 512:] = dot(edge0.reshape(256, 512).astype(BF16), qkv_s[:, 512:]).astype(BF16)
    edge_buf[...] = dot(edge2.reshape(256, 512).astype(BF16), qkv_s[:, 512:]).astype(BF16)
    for w in range(4):
        rows = slice(w * CELLS, (w + 1) * CELLS)
        for g in range(4):
            q = spread_heads(qkv_buf[rows, g * 128 : g * 128 + 128])
            k0 = qkv_buf[rows, 512 + g * 128 : 640 + g * 128]
            v0 = qkv_buf[rows, 1024 + g * 128 : 1152 + g * 128]
            k2 = edge_buf[rows, g * 128 : g * 128 + 128]
            v2 = edge_buf[rows, 512 + g * 128 : 640 + g * 128]
            s = jnp.where(low_j, dot_over(k2, q, 1, 1), dot_over(k0, q, 1, 1))
            s = s * scale + bias_s[g] + (mask_both if w == 3 else mask_col)
            p = soften(s).astype(F32)
            p = jnp.concatenate([jnp.where(low_j, p, 0.0), jnp.where(low_j, 0.0, p)], axis=0)
            v = jnp.concatenate([v2, v0], axis=0)
            heads[rows, g * 128 : g * 128 + 128] = gather_heads(
                dot_over(p.astype(BF16), v, 0, 0)
            ).astype(BF16)
    finish(edge, 256)


def front(features, flat, gains, weights):
    vmem = pl.BlockSpec(memory_space=pltpu.VMEM)
    hbm = pl.BlockSpec(memory_space=pl.ANY)
    dma = pltpu.SemaphoreType.DMA
    return pl.pallas_call(
        front_kernel,
        out_shape=jax.ShapeDtypeStruct((512, 512), BF16),
        in_specs=[vmem] * 3 + [hbm] * 6,
        out_specs=vmem,
        scratch_shapes=[pltpu.VMEM(w.shape, BF16) for w in weights]
        + [
            dma((6,)),
            pltpu.VMEM((4, CELLS, 256), F32),
            pltpu.VMEM((4, CELLS, 256), F32),
            pltpu.VMEM((32, 4, WIN, 512), F32),
            pltpu.VMEM((256, 1536), BF16),
            pltpu.VMEM((256, 1024), BF16),
            pltpu.VMEM((256, 512), BF16),
        ]
        + [pltpu.VMEM((2, 64, 512), BF16)] * 4
        + [dma((2, 2)), dma((2, 2))],
        compiler_params=pltpu.CompilerParams(
            collective_id=0, has_side_effects=True, vmem_limit_bytes=60 * 1024 * 1024
        ),
        name="front",
    )(features, flat, gains, *weights)


def flat_tables(table):
    span = 2 * WIN - 1
    grid = table.reshape(span, span, -1) * LOG2E
    grid = jnp.pad(grid, ((0, 1), (0, 1), (0, 0)))
    return grid.reshape(256, -1).T


def slot_ids(route_row, experts, capacity):
    count = route_row.shape[0]
    onehot = (route_row[:, None] == jnp.arange(experts, dtype=jnp.int32)[None, :]).astype(
        jnp.bfloat16
    )
    order = jnp.arange(count, dtype=jnp.int32)
    earlier = (order[None, :] < order[:, None]).astype(jnp.bfloat16)
    ahead = jnp.dot(earlier, onehot, preferred_element_type=jnp.float32)
    position = jnp.sum(ahead * onehot, axis=-1).astype(jnp.int32)
    return route_row * capacity + position


def regroup(grid):
    rolled = jnp.roll(grid, (-HALF, -HALF), (0, 1))
    parts = rolled.reshape((4, WIN, 2, WIN) + grid.shape[2:])
    return jnp.moveaxis(parts, 2, 0).reshape((-1,) + grid.shape[2:])


def ungroup(tokens):
    parts = tokens.reshape((2, 4, WIN, WIN) + tokens.shape[1:])
    grid = jnp.moveaxis(parts, 0, 2).reshape((32, 16) + tokens.shape[1:])
    return jnp.roll(grid, (HALF, HALF), (0, 1))


def local(
    features,
    routes,
    qkv_regular,
    proj_regular,
    table_regular,
    gain_regular,
    mlp_up,
    mlp_down,
    gain_mlp,
    qkv_shifted,
    proj_shifted,
    table_shifted,
    gain_shifted,
    expert_in,
    expert_out,
    gain_expert,
):
    weight_in = lax.all_gather(expert_in[0], "band", axis=1, tiled=True)
    weight_out = lax.all_gather(expert_out[0], "band", axis=0, tiled=True)
    flat = jnp.concatenate([flat_tables(table_regular), flat_tables(table_shifted)], axis=0)
    gains = jnp.stack([gain_regular, gain_mlp, gain_shifted, gain_expert])
    third_out = front(
        features,
        flat,
        gains,
        (qkv_regular, proj_regular, mlp_up, mlp_down, qkv_shifted, proj_shifted),
    )
    model_width = 512
    experts = lax.axis_size("expert")
    capacity = 32
    route_rows = regroup(routes.reshape(32, 16))
    slots = slot_ids(route_rows, experts, capacity)
    place = (slots[None, :] == jnp.arange(experts * capacity, dtype=jnp.int32)[:, None]).astype(
        jnp.bfloat16
    )
    outgoing = jnp.dot(place, third_out, preferred_element_type=jnp.float32).astype(jnp.bfloat16)
    arrived = lax.all_to_all(
        outgoing.reshape(experts, capacity, model_width),
        "expert",
        split_axis=0,
        concat_axis=0,
        tiled=True,
    ).reshape(experts * capacity, model_width)
    hidden = jax.nn.gelu(
        jnp.dot(arrived, weight_in, preferred_element_type=jnp.float32), approximate=False
    ).astype(jnp.bfloat16)
    rows_out = jnp.dot(hidden, weight_out, preferred_element_type=jnp.float32).astype(jnp.bfloat16)
    returned = lax.all_to_all(
        rows_out.reshape(experts, capacity, model_width),
        "expert",
        split_axis=0,
        concat_axis=0,
        tiled=True,
    ).reshape(experts * capacity, model_width)
    take = (slots[:, None] == jnp.arange(experts * capacity, dtype=jnp.int32)[None, :]).astype(
        jnp.bfloat16
    )
    expert_rows = jnp.dot(take, returned, preferred_element_type=jnp.float32)
    encoded = (
        third_out.astype(jnp.float32) + layer_norm(expert_rows.astype(jnp.float32), gain_expert)
    ).astype(jnp.bfloat16)
    return ungroup(encoded)[None]


def solution(mesh):
    return jax.shard_map(
        local,
        mesh=mesh,
        in_specs=(
            P("expert", None, "band", None),
            P("expert", "band", None, None, None),
        )
        + (P(),) * 11
        + (P("expert", None, "band"), P("expert", "band", None), P()),
        out_specs=P("expert", None, "band", None),
        check_vma=False,
    )
```

profile of v0, /device:TPU:1, one launch (start us, length us, event | category | flops | bytes accessed | tf_op | source)
XLA Modules:
  0.0 134.2 jit_solution(7203833010701346357)
XLA Ops:
  6.5 0.0 all-gather.5.cloned.1.call-start
  6.6 0.7 all-gather.5.cloned.1.call-update
  7.3 0.0 all-gather.7.cloned.1.call-start
  7.3 0.7 all-gather.7.cloned.1.call-update
  8.0 0.8 slice.38
  8.8 0.8 pad_add_fusion.1
  9.6 0.8 slice_add_fusion
  10.4 0.1 reshape.73
  10.4 0.1 copy.22
  10.5 0.1 reshape.74
  10.6 0.7 broadcast_multiply_fusion.1
  11.3 0.1 mul.64
  11.5 0.1 reshape.71
  11.6 0.7 broadcast_multiply_fusion
  12.3 0.1 mul.66
  12.4 0.1 reshape.72
  12.5 0.0 copy-done.4
  12.6 0.0 copy-done.3
  12.6 0.6 pad_maximum_fusion.3.gains_ref
  13.2 0.6 pad_maximum_fusion.2.flat_ref
  13.8 25.0 %front.1 = bf16[512,512]{1,0:T(8,128)(2,1)} custom-call(bf16[1,32,16,512]{3,2,1,0:T(8,128)(2,1)} %x_ref.1, f32[32,256]{1,0:T(8,128)} %pad_maximum_fusion.2.flat_ref, f32[4,512]{1,0:T(4,128)} %pad_maximum_fusion.3.gains_ref, bf16[512,1536]{1,0:T(8,128)(2,1)} %qkv_r_hbm.1, bf16[512,512]{1,0:T(8,128)(2,1)} %proj_r_hbm.1, bf16[512,2048]{1,0:T(8,128)(2,1)} %up_hbm.1, ...), custom_call_target="tpu_custom_call" | custom-call | tf_op jit(solution)/shard_map/front/pallas_call | solution.py:302
  38.8 0.3 fusion.27
  39.1 1.8 %fusion.19 = bf16[1024,512]{1,0:T(8,128)(2,1)S(1)} fusion(bf16[512,512]{1,0:T(8,128)(2,1)} %front.1, s32[512]{0:T(512)S(1)} %convert_add_fusion), kind=kOutput, calls=%fused_computation.27 | convolution fusion | flops 537919488 | bytes 1574912 | tf_op jit(solution)/shard_map/dot_general | solution.py:393
  40.9 25.8 %all_to_all.10 = bf16[32,32,512]{2,1,0:T(8,128)(2,1)S(1)} all-to-all(bf16[32,32,512]{2,1,0:T(8,128)(2,1)S(1)} %bitcast.52), channel_id=1, replica_groups=mesh['band'=4,'expert'=32] {'expert'}, dimensions={0} | all-to-all | bytes 2097152 | tf_op jit(solution)/shard_map/all_to_all | solution.py:394
  66.7 11.5 %all-gather.7.cloned.1.call-done = bf16[1,2048,512]{2,1,0:T(8,128)(2,1)} async-done(((bf16[1,512,512]{2,1,0:T(8,128)(2,1)}), bf16[1,2048,512]{2,1,0:T(8,128)(2,1)}) %all-gather.7.cloned.1.call-update) | async-done | bytes 2097168 | tf_op jit(solution)/shard_map/all_gather | solution.py:376
  78.2 22.0 %fusion.20 = bf16[1024,512]{1,0:T(8,128)(2,1)S(1)} fusion(bf16[1,2048,512]{2,1,0:T(8,128)(2,1)} %all-gather.7.cloned.1.call-done, bf16[1024,512]{1,0:T(8,128)(2,1)S(1)} %bitcast.49, bf16[1,512,2048]{2,1,0:T(8,128)(2,1)} %all-gather.5.cloned.1.call-done), kind=kOutput, calls=%fused_computation.28 | convolution fusion | flops 4431806464 | bytes 6291456 | tf_op jit(solution)/shard_map/dot_general | solution.py:404
  100.1 24.7 %all_to_all.11 = bf16[32,32,512]{2,1,0:T(8,128)(2,1)S(1)} all-to-all(bf16[32,32,512]{2,1,0:T(8,128)(2,1)S(1)} %bitcast.51), channel_id=1, replica_groups=mesh['band'=4,'expert'=32] {'expert'}, dimensions={0} | all-to-all | bytes 2097152 | tf_op jit(solution)/shard_map/all_to_all | solution.py:405
  124.8 0.8 fusion.64
  125.7 0.3 multiply_reduce_fusion
  125.9 0.3 add_convert_fusion
  126.2 0.1 copy.23
  126.3 1.0 fusion.31
  (17 shorter events, 0.1 us)
Async XLA Ops:
  6.5 6.0 %copy-start.4 = (f32[512]{0:T(512)S(1)}, f32[512]{0:T(512)}, u32[]{:S(2)}) copy-start(f32[512]{0:T(512)} %param.21) | copy-start | bytes 6148
  6.5 6.0 %copy-start.3 = (f32[512]{0:T(512)S(1)}, f32[512]{0:T(512)}, u32[]{:S(2)}) copy-start(f32[512]{0:T(512)} %param.24) | copy-start | bytes 6148
  6.5 6.0 %copy-start.2 = (f32[512]{0:T(512)S(1)}, f32[512]{0:T(512)}, u32[]{:S(2)}) copy-start(f32[512]{0:T(512)} %param.28) | copy-start | bytes 6148
  6.5 6.0 %copy-start.1 = (f32[512]{0:T(512)S(1)}, f32[512]{0:T(512)}, u32[]{:S(2)}) copy-start(f32[512]{0:T(512)} %param.31) | copy-start | bytes 6148
  6.5 60.1 %all-gather.5.cloned.1.call-start = ((), (), s32[]{:S(2)}) async-start(), calls=%async_computation.2 | async-start | bytes 2621440 | tf_op jit(solution)/shard_map/all_gather | solution.py:375
  7.3 70.9 %all-gather.7.cloned.1.call-start = ((), (), s32[]{:S(2)}) async-start(), calls=%async_computation.3 | async-start | bytes 2621440 | tf_op jit(solution)/shard_map/all_gather | solution.py:376
  124.8 1.1 copy-start
Sparse Core Ops, SparseCore 0:
  9.0 36.8 all-gather.4
  47.5 30.5 all-gather.6
where the time goes:
time: 135 us; the launch traced here: 134 us
  blocking collectives  50.5 us (37%)
  Pallas kernels  25 us (19%)
  matrix products  24.8 us (18%)
  between operations  13.6 us (10%)
  waiting for transfers between devices  12.9 us (10%)
  other arithmetic  5.81 us (4%)
  local copies, waits for them, and re-layouts  1.58 us (1%)
    all_to_all x1, blocking collectives, local(): lax.all_to_all(outgoing.reshape(experts, capacity, model_width), 'expert'...  25.8 us
    pallas_call x1, Pallas kernels, front(): pl.pallas_call(front_kernel, out_shape=jax.ShapeDtypeStruct((512, 512), B...  25 us
    all_to_all x1, blocking collectives, local(): lax.all_to_all(rows_out.reshape(experts, capacity, model_width), 'expert'...  24.7 us
    dot_general x1, matrix products, local(): jnp.dot(hidden, weight_out, preferred_element_type=jnp.float32)  22 us
    all_gather x1, waiting for transfers between devices, local(): weight_out = lax.all_gather(expert_out[0], 'band', axis=0, tiled=True)  11.5 us
  transfers between devices with their start and end apart: 2, of which 1 were waited for; matrix products, arithmetic and copies ran while one was open for 6% of the time, Pallas kernels for 19%

commit v1 on v0

--- a/solution.py
+++ b/solution.py
@@ -44,15 +44,20 @@
     return lax.broadcasted_iota(jnp.int32, shape, len(shape) - 2) < HALF
 
 
-def window_bias(flat_ref, first_head, bias_ref):
+def window_bias(table_ref, pad_ref, bias_ref):
+    span = 2 * WIN - 1
+    pad_ref[...] = jnp.zeros(pad_ref.shape, F32)
+    for a in range(span):
+        pad_ref[a * 16 : a * 16 + span, 0:16] = table_ref[a * span : a * span + span, :] * LOG2E
+    flat = jnp.transpose(pad_ref[...])
     pitch = 2 * WIN
     width = pitch * pitch
     even = lax.broadcasted_iota(jnp.int32, (WIN, LANES), 1) % pitch < WIN
     for group in range(4):
         for pair in range(2):
-            head = first_head + group * 4 + pair * 2
-            row_even = jnp.broadcast_to(flat_ref[head : head + 1, :], (WIN, width))
-            row_odd = jnp.broadcast_to(flat_ref[head + 1 : head + 2, :], (WIN, width))
+            head = group * 4 + pair * 2
+            row_even = jnp.broadcast_to(flat[head : head + 1, :], (WIN, width))
+            row_odd = jnp.broadcast_to(flat[head + 1 : head + 2, :], (WIN, width))
             for key_row in range(WIN):
                 back = (WIN - 1 - key_row) * pitch + WIN - 1
                 a = pltpu.roll(row_even, (width - back) % width, axis=1, stride=1, stride_axis=0)
@@ -91,15 +96,22 @@
 
 def front_kernel(
     x_ref,
-    flat_ref,
-    gains_ref,
+    table_r_ref,
+    table_s_ref,
+    gain_r_ref,
+    gain_m_ref,
+    gain_s_ref,
     qkv_r_hbm,
     proj_r_hbm,
     up_hbm,
     down_hbm,
     qkv_s_hbm,
     proj_s_hbm,
+    own_in,
+    own_out,
     out_ref,
+    got_in,
+    got_out,
     qkv_r,
     proj_r,
     up,
@@ -107,6 +119,7 @@
     qkv_s,
     proj_s,
     load_sem,
+    pad,
     bias_r,
     bias_s,
     tiles,
@@ -119,6 +132,8 @@
     from_right,
     send_sem,
     recv_sem,
+    shard_send,
+    shard_recv,
 ):
     band = lax.axis_index("band")
     bands = lax.axis_size("band")
@@ -144,9 +159,25 @@
         pl.semaphore_signal(barrier, inc=1, device_id={"band": other}, device_id_type=MESH)
     pl.semaphore_wait(barrier, 2)
 
+    def shard_sends(own, got, first):
+        return [
+            pltpu.make_async_remote_copy(
+                src_ref=own.at[0],
+                dst_ref=got.at[n],
+                send_sem=shard_send.at[first + n],
+                recv_sem=shard_recv.at[first + n],
+                device_id={"band": other},
+                device_id_type=MESH,
+            )
+            for n, other in enumerate((right, left))
+        ]
+
+    for send in shard_sends(own_in, got_in, 0):
+        send.start()
+
     scale = LOG2E * 32**-0.5
-    window_bias(flat_ref, 0, bias_r)
-    window_bias(flat_ref, 16, bias_s)
+    window_bias(table_r_ref, pad, bias_r)
+    window_bias(table_s_ref, pad, bias_s)
     for load in loads[:4]:
         load.wait()
 
@@ -193,12 +224,12 @@
                 heads[rows, g * 128 : g * 128 + 128] = gather_heads(
                     dot_over(soften(s), v, 0, 0)
                 ).astype(BF16)
-        first = (xf + layer_norm(dot(heads[...], proj_r[...]), gains_ref[0:1, :])).astype(BF16)
+        first = (xf + layer_norm(dot(heads[...], proj_r[...]), gain_r_ref[...])).astype(BF16)
         total = jnp.zeros((256, 512), F32)
         for f in range(4):
             hidden = gelu(dot(first, up[:, f * 512 : f * 512 + 512])).astype(BF16)
             total = total + dot(hidden, down[f * 512 : f * 512 + 512, :])
-        second = (first.astype(F32) + layer_norm(total, gains_ref[1:2, :])).astype(BF16).astype(F32)
+        second = (first.astype(F32) + layer_norm(total, gain_m_ref[...])).astype(BF16).astype(F32)
         for r in range(2):
             rows = pl.ds(part * 16 + r * 8, 8)
             w0 = second[r * 128 : r * 128 + 64].reshape(WIN, WIN, 512)
@@ -216,6 +247,8 @@
         return carry
 
     lax.fori_loop(0, 2, first_part, 0)
+    for send in shard_sends(own_out, got_out, 2):
+        send.start()
 
     def shifted(column):
         pieces = []
@@ -227,7 +260,7 @@
         return jnp.concatenate(pieces, axis=0)
 
     def finish(x, first_row):
-        third = x + layer_norm(dot(heads[...], proj_s[...]), gains_ref[2:3, :])
+        third = x + layer_norm(dot(heads[...], proj_s[...]), gain_s_ref[...])
         out_ref[first_row : first_row + 256, :] = third.astype(BF16)
 
     key = lax.broadcasted_iota(jnp.int32, (CELLS, 256), 0)
@@ -293,20 +326,24 @@
                 dot_over(p.astype(BF16), v, 0, 0)
             ).astype(BF16)
     finish(edge, 256)
-
-
-def front(features, flat, gains, weights):
+    for send in shard_sends(own_in, got_in, 0) + shard_sends(own_out, got_out, 2):
+        send.wait()
+
+
+def front(features, tables, gains, weights, shards):
     vmem = pl.BlockSpec(memory_space=pltpu.VMEM)
     hbm = pl.BlockSpec(memory_space=pl.ANY)
     dma = pltpu.SemaphoreType.DMA
+    pair = jax.ShapeDtypeStruct((2, 512, 512), BF16)
     return pl.pallas_call(
         front_kernel,
-        out_shape=jax.ShapeDtypeStruct((512, 512), BF16),
-        in_specs=[vmem] * 3 + [hbm] * 6,
-        out_specs=vmem,
+        out_shape=(jax.ShapeDtypeStruct((512, 512), BF16), pair, pair),
+        in_specs=[vmem] * 6 + [hbm] * 8,
+        out_specs=(vmem, hbm, hbm),
         scratch_shapes=[pltpu.VMEM(w.shape, BF16) for w in weights]
         + [
             dma((6,)),
+            pltpu.VMEM((256, 128), F32),
             pltpu.VMEM((4, CELLS, 256), F32),
             pltpu.VMEM((4, CELLS, 256), F32),
             pltpu.VMEM((32, 4, WIN, 512), F32),
@@ -315,43 +352,234 @@
             pltpu.VMEM((256, 512), BF16),
         ]
         + [pltpu.VMEM((2, 64, 512), BF16)] * 4
-        + [dma((2, 2)), dma((2, 2))],
+        + [dma((2, 2)), dma((2, 2)), dma((4,)), dma((4,))],
         compiler_params=pltpu.CompilerParams(
             collective_id=0, has_side_effects=True, vmem_limit_bytes=60 * 1024 * 1024
         ),
         name="front",
-    )(features, flat, gains, *weights)
-
-
-def flat_tables(table):
-    span = 2 * WIN - 1
-    grid = table.reshape(span, span, -1) * LOG2E
-    grid = jnp.pad(grid, ((0, 1), (0, 1), (0, 0)))
-    return grid.reshape(256, -1).T
-
-
-def slot_ids(route_row, experts, capacity):
-    count = route_row.shape[0]
-    onehot = (route_row[:, None] == jnp.arange(experts, dtype=jnp.int32)[None, :]).astype(
-        jnp.bfloat16
+    )(features, *tables, *gains, *weights, *shards)
+
+
+AWAY = sorted(
+    ((z, x) for z in range(4) for x in range(4)),
+    key=lambda d: (min(d[0], 4 - d[0]) + min(d[1], 4 - d[1]), d),
+)
+PEERS = 32
+CAP = 32
+GROUPS = 4
+PER_GROUP = PEERS // GROUPS
+ROWS = PER_GROUP * CAP
+
+
+def moe_kernel(
+    third_ref,
+    routes_ref,
+    gain_ref,
+    own_in,
+    own_out,
+    got_in,
+    got_out,
+    enc_ref,
+    w_in,
+    w_out,
+    load_sem,
+    outgoing,
+    arrived,
+    total,
+    result,
+    returned,
+    take,
+    go_send,
+    go_recv,
+    back_send,
+    back_recv,
+    far_send,
+    far_recv,
+):
+    band = lax.axis_index("band")
+    bands = lax.axis_size("band")
+    right = lax.rem(band + 1, bands)
+    left = lax.rem(band + bands - 1, bands)
+    me = lax.axis_index("expert")
+    my_z, my_x, my_core = me // 8, (me // 2) % 4, me % 2
+
+    def peer(place, sign):
+        z, x = AWAY[place // 2]
+        return (
+            (my_z + 4 + sign * z) % 4 * 4 + (my_x + 4 + sign * x) % 4
+        ) * 2 + (my_core + place % 2) % 2
+
+    barrier = pltpu.get_barrier_semaphore()
+    for place in range(1, PEERS):
+        pl.semaphore_signal(
+            barrier, inc=1, device_id={"expert": peer(place, 1)}, device_id_type=MESH
+        )
+    for other in (left, right):
+        pl.semaphore_signal(barrier, inc=1, device_id={"band": other}, device_id_type=MESH)
+
+    loads = [
+        pltpu.make_async_copy(src, dst, load_sem.at[n])
+        for n, (src, dst) in enumerate(
+            (
+                (own_in.at[0], w_in.at[0]),
+                (own_out.at[0], w_out.at[0]),
+                (got_in.at[0], w_in.at[1]),
+                (got_out.at[0], w_out.at[1]),
+                (got_in.at[1], w_in.at[2]),
+                (got_out.at[1], w_out.at[2]),
+            )
+        )
+    ]
+    for load in loads:
+        load.start()
+    fars = [
+        pltpu.make_async_remote_copy(
+            src_ref=src,
+            dst_ref=dst.at[3],
+            send_sem=far_send.at[n],
+            recv_sem=far_recv.at[n],
+            device_id={"band": other},
+            device_id_type=MESH,
+        )
+        for n, (src, dst, other) in enumerate(
+            ((got_in.at[0], w_in, right), (got_out.at[1], w_out, left))
+        )
+    ]
+    goes = [
+        pltpu.make_async_remote_copy(
+            src_ref=outgoing.at[place],
+            dst_ref=arrived.at[place],
+            send_sem=go_send.at[place],
+            recv_sem=go_recv.at[place],
+            device_id={"expert": peer(place, 1)},
+            device_id_type=MESH,
+        )
+        for place in range(1, PEERS)
+    ]
+    backs = [
+        pltpu.make_async_remote_copy(
+            src_ref=result.at[place],
+            dst_ref=returned.at[place],
+            send_sem=back_send.at[place],
+            recv_sem=back_recv.at[place],
+            device_id={"expert": peer(place, -1)},
+            device_id_type=MESH,
+        )
+        for place in range(1, PEERS)
+    ]
+
+    routes = routes_ref[...]
+    code = (((routes >> 3) - my_z) & 3) * 4 + (((routes >> 1) - my_x) & 3)
+    spot = jnp.zeros_like(routes)
+    for n, (z, x) in enumerate(AWAY):
+        spot = jnp.where(code == z * 4 + x, n, spot)
+    spot = spot * 2 + ((routes - my_core) & 1)
+    chosen = lax.broadcasted_iota(jnp.int32, (PEERS, 512), 0) == spot
+    onehot = jnp.where(chosen, 1.0, 0.0)
+    before = lax.broadcasted_iota(jnp.int32, (512, 512), 0) < lax.broadcasted_iota(
+        jnp.int32, (512, 512), 1
     )
-    order = jnp.arange(count, dtype=jnp.int32)
-    earlier = (order[None, :] < order[:, None]).astype(jnp.bfloat16)
-    ahead = jnp.dot(earlier, onehot, preferred_element_type=jnp.float32)
-    position = jnp.sum(ahead * onehot, axis=-1).astype(jnp.int32)
-    return route_row * capacity + position
+    ahead = dot(onehot.astype(BF16), jnp.where(before, 1.0, 0.0).astype(BF16))
+    slot = spot.astype(F32) * CAP + jnp.sum(onehot * ahead, axis=0, keepdims=True)
+
+    third = third_ref[...]
+    for g in range(GROUPS):
+        rows = (lax.broadcasted_iota(jnp.int32, (ROWS, 512), 0) + g * ROWS).astype(F32)
+        place = jnp.where(rows == slot, 1.0, 0.0).astype(BF16)
+        block = dot(place, third).astype(BF16).reshape(PER_GROUP, CAP, 512)
+        if g == 0:
+            arrived[0] = block[0]
+            outgoing[1:PER_GROUP] = block[1:]
+        else:
+            outgoing[g * PER_GROUP : (g + 1) * PER_GROUP] = block
+        if g == 0:
+            pl.semaphore_wait(barrier, PEERS - 1 + 2)
+            for far in fars:
+                far.start()
+        for go in goes[max(g * PER_GROUP - 1, 0) : (g + 1) * PER_GROUP - 1]:
+            go.start()
+
+    slot_column = jnp.transpose(jnp.broadcast_to(slot, (LANES, 512)))
+    lane = lax.broadcasted_iota(jnp.int32, (512, LANES), 1).astype(F32)
+    for n in range(PEERS * CAP // LANES):
+        take[:, n * LANES : (n + 1) * LANES] = jnp.where(
+            slot_column == lane + n * LANES, 1.0, 0.0
+        ).astype(BF16)
+
+    def layer(rows, n):
+        hidden = gelu(dot(rows, w_in[n])).astype(BF16)
+        return dot(hidden, w_out[n])
+
+    for load in loads:
+        load.wait()
+    for g in range(GROUPS):
+        for go in goes[max(g * PER_GROUP - 1, 0) : (g + 1) * PER_GROUP - 1]:
+            go.wait_recv()
+        rows = arrived[g * PER_GROUP : (g + 1) * PER_GROUP].reshape(ROWS, 512)
+        total[g * ROWS : (g + 1) * ROWS] = layer(rows, 0) + layer(rows, 1) + layer(rows, 2)
+    for far in fars:
+        far.wait()
+    for g in range(GROUPS):
+        rows = arrived[g * PER_GROUP : (g + 1) * PER_GROUP].reshape(ROWS, 512)
+        block = (total[g * ROWS : (g + 1) * ROWS] + layer(rows, 3)).astype(BF16)
+        block = block.reshape(PER_GROUP, CAP, 512)
+        if g == 0:
+            returned[0] = block[0]
+            result[1:PER_GROUP] = block[1:]
+        else:
+            result[g * PER_GROUP : (g + 1) * PER_GROUP] = block
+        for back in backs[max(g * PER_GROUP - 1, 0) : (g + 1) * PER_GROUP - 1]:
+            back.start()
+    for go in goes:
+        go.wait_send()
+    for back in backs:
+        back.wait()
+    rows = dot(take[...], returned[...].reshape(PEERS * CAP, 512))
+    encoded = third.astype(F32) + layer_norm(rows, gain_ref[...])
+    low_cell = cell_is_low((1, WIN, 512))
+    for w in range(4):
+        mid = encoded[w * CELLS : (w + 1) * CELLS].reshape(WIN, WIN, 512)
+        edge = encoded[256 + w * CELLS : 256 + (w + 1) * CELLS].reshape(WIN, WIN, 512)
+        w0 = turn(jnp.where(low_cell, mid, edge))
+        w1 = turn(jnp.where(low_cell, edge, mid))
+        block = jnp.concatenate([w0, w1], axis=1).astype(BF16)
+        for half in range(2):
+            top = (w * 8 + 4 + half * 4) % 32
+            enc_ref[0, top : top + 4] = block[half * 4 : half * 4 + 4]
+
+
+def moe(third, routes, gain, shards, got):
+    vmem = pl.BlockSpec(memory_space=pltpu.VMEM)
+    hbm = pl.BlockSpec(memory_space=pl.ANY)
+    dma = pltpu.SemaphoreType.DMA
+    return pl.pallas_call(
+        moe_kernel,
+        out_shape=jax.ShapeDtypeStruct((1, 32, 16, 512), BF16),
+        in_specs=[vmem] * 3 + [hbm] * 4,
+        out_specs=vmem,
+        scratch_shapes=[
+            pltpu.VMEM((4, 512, 512), BF16),
+            pltpu.VMEM((4, 512, 512), BF16),
+            dma((6,)),
+            pltpu.VMEM((PEERS, CAP, 512), BF16),
+            pltpu.VMEM((PEERS, CAP, 512), BF16),
+            pltpu.VMEM((PEERS * CAP, 512), F32),
+            pltpu.VMEM((PEERS, CAP, 512), BF16),
+            pltpu.VMEM((PEERS, CAP, 512), BF16),
+            pltpu.VMEM((512, PEERS * CAP), BF16),
+        ]
+        + [dma((PEERS,))] * 4
+        + [dma((2,))] * 2,
+        compiler_params=pltpu.CompilerParams(
+            collective_id=1, has_side_effects=True, vmem_limit_bytes=60 * 1024 * 1024
+        ),
+        name="moe",
+    )(third, routes, gain, *shards, *got)
 
 
 def regroup(grid):
     rolled = jnp.roll(grid, (-HALF, -HALF), (0, 1))
-    parts = rolled.reshape((4, WIN, 2, WIN) + grid.shape[2:])
-    return jnp.moveaxis(parts, 2, 0).reshape((-1,) + grid.shape[2:])
-
-
-def ungroup(tokens):
-    parts = tokens.reshape((2, 4, WIN, WIN) + tokens.shape[1:])
-    grid = jnp.moveaxis(parts, 0, 2).reshape((32, 16) + tokens.shape[1:])
-    return jnp.roll(grid, (HALF, HALF), (0, 1))
+    return rolled.reshape(4, WIN, 2, WIN).transpose(2, 0, 1, 3)
 
 
 def local(
@@ -372,51 +600,16 @@
     expert_out,
     gain_expert,
 ):
-    weight_in = lax.all_gather(expert_in[0], "band", axis=1, tiled=True)
-    weight_out = lax.all_gather(expert_out[0], "band", axis=0, tiled=True)
-    flat = jnp.concatenate([flat_tables(table_regular), flat_tables(table_shifted)], axis=0)
-    gains = jnp.stack([gain_regular, gain_mlp, gain_shifted, gain_expert])
-    third_out = front(
+    shards = (expert_in, expert_out)
+    third, *got = front(
         features,
-        flat,
-        gains,
+        (table_regular, table_shifted),
+        [g.reshape(1, 512) for g in (gain_regular, gain_mlp, gain_shifted)],
         (qkv_regular, proj_regular, mlp_up, mlp_down, qkv_shifted, proj_shifted),
+        shards,
     )
-    model_width = 512
-    experts = lax.axis_size("expert")
-    capacity = 32
-    route_rows = regroup(routes.reshape(32, 16))
-    slots = slot_ids(route_rows, experts, capacity)
-    place = (slots[None, :] == jnp.arange(experts * capacity, dtype=jnp.int32)[:, None]).astype(
-        jnp.bfloat16
-    )
-    outgoing = jnp.dot(place, third_out, preferred_element_type=jnp.float32).astype(jnp.bfloat16)
-    arrived = lax.all_to_all(
-        outgoing.reshape(experts, capacity, model_width),
-        "expert",
-        split_axis=0,
-        concat_axis=0,
-        tiled=True,
-    ).reshape(experts * capacity, model_width)
-    hidden = jax.nn.gelu(
-        jnp.dot(arrived, weight_in, preferred_element_type=jnp.float32), approximate=False
-    ).astype(jnp.bfloat16)
-    rows_out = jnp.dot(hidden, weight_out, preferred_element_type=jnp.float32).astype(jnp.bfloat16)
-    returned = lax.all_to_all(
-        rows_out.reshape(experts, capacity, model_width),
-        "expert",
-        split_axis=0,
-        concat_axis=0,
-        tiled=True,
-    ).reshape(experts * capacity, model_width)
-    take = (slots[:, None] == jnp.arange(experts * capacity, dtype=jnp.int32)[None, :]).astype(
-        jnp.bfloat16
-    )
-    expert_rows = jnp.dot(take, returned, preferred_element_type=jnp.float32)
-    encoded = (
-        third_out.astype(jnp.float32) + layer_norm(expert_rows.astype(jnp.float32), gain_expert)
-    ).astype(jnp.bfloat16)
-    return ungroup(encoded)[None]
+    order = regroup(routes.reshape(32, 16)).reshape(1, 512)
+    return moe(third, order, gain_expert.reshape(1, 512), shards, got)
 
 
 def solution(mesh):

time: 135 us -> 84 us (0.62)
  Pallas kernels: 25 us -> 75.6 us
  blocking collectives: 50.5 us -> 0 us
  matrix products: 24.8 us -> 0 us
  between operations: 13.6 us -> 0.02 us
  waiting for transfers between devices: 12.9 us -> 0 us
  local copies, waits for them, and re-layouts: 1.58 us -> 6.4 us
  other arithmetic: 5.81 us -> 1.55 us
    pallas_call x1 -> x2, Pallas kernels: 25 us -> 75.6 us  [the longest x1 43.7 us: moe(): pl.pallas_call(moe_kernel, out_shape=jax.ShapeDtypeStruct((1, 32, 16, 512...]
    all_to_all x2 -> x0, blocking collectives: 50.5 us -> none  [the longest x1 25.8 us: local(): lax.all_to_all(outgoing.reshape(experts, capacity, model_width), 'expert'...]
    dot_general x4 -> x0, matrix products: 24.8 us -> none  [the longest x1 22 us: local(): jnp.dot(hidden, weight_out, preferred_element_type=jnp.float32)]
    all_gather x2 -> x0, waiting for transfers between devices: 11.5 us -> none  [the longest x1 11.5 us: local(): weight_out = lax.all_gather(expert_out[0], 'band', axis=0, tiled=True)]
    unnamed x10 -> x3, local copies, waits for them, and re-layouts: 0.02 us -> 4.78 us
    mul x2 -> x0, other arithmetic: 1.45 us -> none  [flat_tables(): grid = table.reshape(span, span, -1) * LOG2E]
    unnamed x2 -> x0, waiting for transfers between devices: 1.38 us -> none
  transfers between devices with their start and end apart: 2 -> 0, of which waited for: 1 -> 0; matrix products, arithmetic and copies ran while one was open for 6% -> 0% of each run, Pallas kernels for 19% -> 0%
where the time goes in v1:
time: 84 us; the launch traced here: 83.6 us
  Pallas kernels  75.6 us (90%)
  local copies, waits for them, and re-layouts  6.4 us (8%)
  other arithmetic  1.55 us (2%)
    pallas_call x1, Pallas kernels, moe(): pl.pallas_call(moe_kernel, out_shape=jax.ShapeDtypeStruct((1, 32, 16, 512...  43.7 us
    pallas_call x1, Pallas kernels, front(): pl.pallas_call(front_kernel, out_shape=(jax.ShapeDtypeStruct((512, 512),...  31.9 us
    unnamed x3, local copies, waits for them, and re-layouts  4.78 us

profile of v1, /device:TPU:1, one launch (start us, length us, event | category | flops | bytes accessed | tf_op | source)
XLA Modules:
  0.0 83.6 jit_solution(1614064402408378121)
XLA Ops:
  0.0 0.8 slice.22
  0.8 0.8 pad_add_fusion.1
  1.5 0.8 slice_add_fusion
  2.3 0.1 reshape.24
  2.4 0.1 copy.21
  2.5 0.7 reshape.25.routes_ref
  3.2 1.5 %copy.17.table_r_ref = f32[225,16]{1,0:T(8,128)} copy(f32[225,16]{0,1:T(8,128)} %param.20) | data formatting | bytes 28800 | tf_op args[4]
  4.6 1.5 %copy.18.table_s_ref = f32[225,16]{1,0:T(8,128)} copy(f32[225,16]{0,1:T(8,128)} %param.27) | data formatting | bytes 28800 | tf_op args[11]
  6.1 31.9 %front.1 = (bf16[512,512]{1,0:T(8,128)(2,1)}, bf16[2,512,512]{2,1,0:T(8,128)(2,1)}, bf16[2,512,512]{2,1,0:T(8,128)(2,1)}) custom-call(bf16[1,32,16,512]{3,2,1,0:T(8,128)(2,1)} %x_ref.1, f32[225,16]{1,0:T(8,128)} %copy.17.table_r_ref, f32[225,16]{1,0:T(8,128)} %copy.18.table_s_ref, f32[1,512]{1,0:T(1,128)} %bitcast.18, f32[1,512]{1,0:T(1,128)} %bitcast.19, ...), custom_call_target="tpu_custom_call" | custom-call | tf_op jit(solution)/shard_map/front/pallas_call | solution.py:338
  38.0 43.7 %moe.1 = bf16[1,32,16,512]{3,2,1,0:T(8,128)(2,1)} custom-call(bf16[512,512]{1,0:T(8,128)(2,1)} %get-tuple-element.8.third_ref, s32[1,512]{1,0:T(1,128)} %reshape.25.routes_ref, f32[1,512]{1,0:T(1,128)} %bitcast.17, bf16[1,512,512]{2,1,0:T(8,128)(2,1)} %own_in.3, bf16[1,512,512]{2,1,0:T(8,128)(2,1)} %own_out.3, bf16[2,512,512]{2,1,0:T(8,128)(2,1)} %get-tuple-element.9.got_in, ...), custom_call_target="tpu_custom_call" | custom-call | tf_op jit(solution)/shard_map/moe/pallas_call | solution.py:555
  81.7 1.9 %copy.24 = bf16[1,32,16,512]{3,2,1,0:T(8,128)(2,1)} copy(bf16[1,32,16,512]{3,2,1,0:T(8,128)(2,1)} %moe.1) | data formatting | bytes 1048576
  (1 shorter events, 0.0 us)

commit v2 on v0

--- a/solution.py
+++ b/solution.py
@@ -44,15 +44,23 @@
     return lax.broadcasted_iota(jnp.int32, shape, len(shape) - 2) < HALF
 
 
-def window_bias(flat_ref, first_head, bias_ref):
+def window_bias(table_ref, pad_ref, bias_ref):
+    span = 2 * WIN - 1
     pitch = 2 * WIN
     width = pitch * pitch
+    pad_ref[...] = jnp.zeros(pad_ref.shape, F32)
+    pad_ref[:, : span * span] = table_ref[...] * LOG2E
+    packed = pad_ref[...]
+    line = lax.broadcasted_iota(jnp.int32, packed.shape, 1) // pitch
+    flat = packed
+    for a in range(1, span):
+        flat = jnp.where(line == a, pltpu.roll(packed, a, axis=1), flat)
     even = lax.broadcasted_iota(jnp.int32, (WIN, LANES), 1) % pitch < WIN
     for group in range(4):
         for pair in range(2):
-            head = first_head + group * 4 + pair * 2
-            row_even = jnp.broadcast_to(flat_ref[head : head + 1, :], (WIN, width))
-            row_odd = jnp.broadcast_to(flat_ref[head + 1 : head + 2, :], (WIN, width))
+            head = group * 4 + pair * 2
+            row_even = jnp.broadcast_to(flat[head : head + 1, :], (WIN, width))
+            row_odd = jnp.broadcast_to(flat[head + 1 : head + 2, :], (WIN, width))
             for key_row in range(WIN):
                 back = (WIN - 1 - key_row) * pitch + WIN - 1
                 a = pltpu.roll(row_even, (width - back) % width, axis=1, stride=1, stride_axis=0)
@@ -89,17 +97,48 @@
     return (e * (1.0 / jnp.sum(e, axis=0, keepdims=True))).astype(BF16)
 
 
-def front_kernel(
+AWAY = sorted(
+    ((z, x) for z in range(4) for x in range(4)),
+    key=lambda d: (min(d[0], 4 - d[0]) + min(d[1], 4 - d[1]), d),
+)
+PEERS = 32
+CAP = 32
+GROUPS = 4
+PER_GROUP = PEERS // GROUPS
+ROWS = PER_GROUP * CAP
+
+
+def token_routes(routes_ref):
+    grid = routes_ref[...].reshape(16, 32).astype(F32).astype(BF16)
+    token = lax.broadcasted_iota(jnp.int32, (32, 512), 1)
+    row = ((token // 64) % 4 * 8 + 4 + (token // 8) % 8) % 32
+    at_row = jnp.where(lax.broadcasted_iota(jnp.int32, (32, 512), 0) == row, 1.0, 0.0)
+    token = lax.broadcasted_iota(jnp.int32, (16, 512), 1)
+    cell = token % 8
+    column = jnp.where(token < 256, HALF + cell, (cell + 12) % 16)
+    at_column = lax.broadcasted_iota(jnp.int32, (16, 512), 0) == column
+    picked = jnp.where(at_column, dot(grid, at_row.astype(BF16)), 0.0)
+    return jnp.sum(picked, axis=0, keepdims=True).astype(jnp.int32)
+
+
+def kernel(
     x_ref,
-    flat_ref,
-    gains_ref,
+    routes_ref,
+    table_r_ref,
+    table_s_ref,
+    gain_r_ref,
+    gain_m_ref,
+    gain_s_ref,
+    gain_e_ref,
     qkv_r_hbm,
     proj_r_hbm,
     up_hbm,
     down_hbm,
     qkv_s_hbm,
     proj_s_hbm,
-    out_ref,
+    own_in,
+    own_out,
+    enc_ref,
     qkv_r,
     proj_r,
     up,
@@ -107,23 +146,54 @@
     qkv_s,
     proj_s,
     load_sem,
+    pad,
     bias_r,
     bias_s,
     tiles,
     qkv_buf,
     edge_buf,
     heads,
+    third_buf,
     to_left,
     to_right,
     from_left,
     from_right,
     send_sem,
     recv_sem,
+    shard_send,
+    shard_recv,
+    w_in,
+    w_out,
+    place,
+    take,
+    outgoing,
+    arrived,
+    result,
+    returned,
+    go_send,
+    go_recv,
+    back_send,
+    back_recv,
 ):
     band = lax.axis_index("band")
     bands = lax.axis_size("band")
     right = lax.rem(band + 1, bands)
     left = lax.rem(band + bands - 1, bands)
+    me = lax.axis_index("expert")
+    my_z, my_x, my_core = me // 8, (me // 2) % 4, me % 2
+
+    def peer(n, sign):
+        z, x = AWAY[n // 2]
+        return (
+            (my_z + 4 + sign * z) % 4 * 4 + (my_x + 4 + sign * x) % 4
+        ) * 2 + (my_core + n % 2) % 2
+
+    barrier = pltpu.get_barrier_semaphore()
+    for n in range(1, PEERS):
+        pl.semaphore_signal(barrier, inc=1, device_id={"expert": peer(n, 1)}, device_id_type=MESH)
+    for other in (left, right):
+        pl.semaphore_signal(barrier, inc=1, device_id={"band": other}, device_id_type=MESH)
+
     loads = [
         pltpu.make_async_copy(src, dst, load_sem.at[n])
         for n, (src, dst) in enumerate(
@@ -134,39 +204,92 @@
                 (down_hbm, down),
                 (qkv_s_hbm, qkv_s),
                 (proj_s_hbm, proj_s),
+                (own_in.at[0], w_in.at[0]),
+                (own_out.at[0], w_out.at[0]),
             )
         )
     ]
     for load in loads:
         load.start()
-    barrier = pltpu.get_barrier_semaphore()
-    for other in (left, right):
-        pl.semaphore_signal(barrier, inc=1, device_id={"band": other}, device_id_type=MESH)
-    pl.semaphore_wait(barrier, 2)
-
+
+    def remote(src, dst, send_sem, recv_sem, to):
+        return pltpu.make_async_remote_copy(
+            src_ref=src,
+            dst_ref=dst,
+            send_sem=send_sem,
+            recv_sem=recv_sem,
+            device_id=to,
+            device_id_type=MESH,
+        )
+
+    def shard(n):
+        to = {"band": left if n % 2 else right}
+        if n < 2:
+            src, dst = own_in.at[0], w_in.at[1 + n]
+        elif n < 6:
+            rows = pl.ds((n // 2 - 1) * 256, 256)
+            src, dst = own_out.at[0, rows], w_out.at[1 + n % 2, rows]
+        elif n == 6:
+            src, dst = w_in.at[1], w_in.at[3]
+        else:
+            src, dst = w_out.at[2], w_out.at[3]
+        return remote(src, dst, shard_send.at[n], shard_recv.at[n], to)
+
+    def go(n):
+        to = {"expert": peer(n, 1)}
+        return remote(outgoing.at[n], arrived.at[n], go_send.at[n], go_recv.at[n], to)
+
+    def back(n):
+        to = {"expert": peer(n, -1)}
+        return remote(result.at[n], returned.at[n], back_send.at[n], back_recv.at[n], to)
+
+    routes = token_routes(routes_ref)
+    code = (((routes >> 3) - my_z) & 3) * 4 + (((routes >> 1) - my_x) & 3)
+    spot = jnp.zeros_like(routes)
+    for n, (z, x) in enumerate(AWAY):
+        spot = jnp.where(code == z * 4 + x, n, spot)
+    spot = spot * 2 + ((routes - my_core) & 1)
+    chosen = lax.broadcasted_iota(jnp.int32, (PEERS, 512), 0) == spot
+    onehot = jnp.where(chosen, 1.0, 0.0)
+    before = lax.broadcasted_iota(jnp.int32, (512, 512), 0) < lax.broadcasted_iota(
+        jnp.int32, (512, 512), 1
+    )
+    ahead = dot(onehot.astype(BF16), jnp.where(before, 1.0, 0.0).astype(BF16))
+    slot = spot.astype(F32) * CAP + jnp.sum(onehot * ahead, axis=0, keepdims=True)
+    for g in range(GROUPS):
+        rows = (lax.broadcasted_iota(jnp.int32, (ROWS, 512), 0) + g * ROWS).astype(F32)
+        place[g * ROWS : (g + 1) * ROWS] = jnp.where(rows == slot, 1.0, 0.0).astype(BF16)
+    slot_column = jnp.transpose(jnp.broadcast_to(slot, (LANES, 512)))
+    lane = lax.broadcasted_iota(jnp.int32, (512, LANES), 1).astype(F32)
+    for n in range(PEERS * CAP // LANES):
+        take[:, n * LANES : (n + 1) * LANES] = jnp.where(
+            slot_column == lane + n * LANES, 1.0, 0.0
+        ).astype(BF16)
     scale = LOG2E * 32**-0.5
-    window_bias(flat_ref, 0, bias_r)
-    window_bias(flat_ref, 16, bias_s)
+    window_bias(table_r_ref, pad, bias_r)
+    window_bias(table_s_ref, pad, bias_s)
+
+    pl.semaphore_wait(barrier, PEERS - 1 + 2)
+    for n in range(2):
+        shard(n).start()
     for load in loads[:4]:
         load.wait()
 
     def sends(part):
         return [
-            pltpu.make_async_remote_copy(
-                src_ref=to_left.at[part],
-                dst_ref=from_right.at[part],
-                send_sem=send_sem.at[0, part],
-                recv_sem=recv_sem.at[0, part],
-                device_id={"band": left},
-                device_id_type=MESH,
+            remote(
+                to_left.at[part],
+                from_right.at[part],
+                send_sem.at[0, part],
+                recv_sem.at[0, part],
+                {"band": left},
             ),
-            pltpu.make_async_remote_copy(
-                src_ref=to_right.at[part],
-                dst_ref=from_left.at[part],
-                send_sem=send_sem.at[1, part],
-                recv_sem=recv_sem.at[1, part],
-                device_id={"band": right},
-                device_id_type=MESH,
+            remote(
+                to_right.at[part],
+                from_left.at[part],
+                send_sem.at[1, part],
+                recv_sem.at[1, part],
+                {"band": right},
             ),
         ]
 
@@ -193,12 +316,12 @@
                 heads[rows, g * 128 : g * 128 + 128] = gather_heads(
                     dot_over(soften(s), v, 0, 0)
                 ).astype(BF16)
-        first = (xf + layer_norm(dot(heads[...], proj_r[...]), gains_ref[0:1, :])).astype(BF16)
+        first = (xf + layer_norm(dot(heads[...], proj_r[...]), gain_r_ref[...])).astype(BF16)
         total = jnp.zeros((256, 512), F32)
         for f in range(4):
             hidden = gelu(dot(first, up[:, f * 512 : f * 512 + 512])).astype(BF16)
             total = total + dot(hidden, down[f * 512 : f * 512 + 512, :])
-        second = (first.astype(F32) + layer_norm(total, gains_ref[1:2, :])).astype(BF16).astype(F32)
+        second = (first.astype(F32) + layer_norm(total, gain_m_ref[...])).astype(BF16).astype(F32)
         for r in range(2):
             rows = pl.ds(part * 16 + r * 8, 8)
             w0 = second[r * 128 : r * 128 + 64].reshape(WIN, WIN, 512)
@@ -213,9 +336,19 @@
             )
         for send in sends(part):
             send.start()
+
+        @pl.when(part == 0)
+        def _():
+            for n in (2, 3):
+                shard(n).start()
+
         return carry
 
     lax.fori_loop(0, 2, first_part, 0)
+    for n in (4, 5):
+        shard(n).start()
+    shard(0).wait_recv()
+    shard(6).start()
 
     def shifted(column):
         pieces = []
@@ -227,8 +360,8 @@
         return jnp.concatenate(pieces, axis=0)
 
     def finish(x, first_row):
-        third = x + layer_norm(dot(heads[...], proj_s[...]), gains_ref[2:3, :])
-        out_ref[first_row : first_row + 256, :] = third.astype(BF16)
+        third = x + layer_norm(dot(heads[...], proj_s[...]), gain_s_ref[...])
+        third_buf[first_row : first_row + 256, :] = third.astype(BF16)
 
     key = lax.broadcasted_iota(jnp.int32, (CELLS, 256), 0)
     lane = lax.broadcasted_iota(jnp.int32, (CELLS, 256), 1)
@@ -241,7 +374,7 @@
     mask_col = jnp.where(col_apart, -100.0 * LOG2E, 0.0)
     mask_both = jnp.where(row_apart | col_apart, -100.0 * LOG2E, 0.0)
 
-    for load in loads[4:]:
+    for load in loads[4:6]:
         load.wait()
     mid = shifted(1).reshape(256, 512)
     qkv_buf[...] = dot(mid.astype(BF16), qkv_s[...]).astype(BF16)
@@ -294,64 +427,111 @@
             ).astype(BF16)
     finish(edge, 256)
 
-
-def front(features, flat, gains, weights):
+    groups = range(GROUPS)[::-1]
+
+    def places(g):
+        return range(max(g * PER_GROUP, 1), (g + 1) * PER_GROUP)[::-1]
+
+    third = third_buf[...]
+    for g in groups:
+        block = dot(place[g * ROWS : (g + 1) * ROWS], third).astype(BF16)
+        block = block.reshape(PER_GROUP, CAP, 512)
+        if g == 0:
+            arrived[0] = block[0]
+            outgoing[1:PER_GROUP] = block[1:]
+        else:
+            outgoing[g * PER_GROUP : (g + 1) * PER_GROUP] = block
+        for n in places(g):
+            go(n).start()
+
+    for n in (3, 5):
+        shard(n).wait_recv()
+    shard(7).start()
+    for n in (1, 2, 4):
+        shard(n).wait_recv()
+    for load in loads[6:]:
+        load.wait()
+
+    def layer(rows, n):
+        hidden = gelu(dot(rows, w_in[n])).astype(BF16)
+        return dot(hidden, w_out[n])
+
+    for g in groups:
+        for n in places(g):
+            go(n).wait_recv()
+        rows = arrived[g * PER_GROUP : (g + 1) * PER_GROUP].reshape(ROWS, 512)
+        total = layer(rows, 0) + layer(rows, 1) + layer(rows, 2)
+        if g == GROUPS - 1:
+            for n in (6, 7):
+                shard(n).wait_recv()
+        block = (total + layer(rows, 3)).astype(BF16).reshape(PER_GROUP, CAP, 512)
+        if g == 0:
+            returned[0] = block[0]
+            result[1:PER_GROUP] = block[1:]
+        else:
+            result[g * PER_GROUP : (g + 1) * PER_GROUP] = block
+        for n in places(g):
+            back(n).start()
+    for n in range(8):
+        shard(n).wait_send()
+    rows = jnp.zeros((512, 512), F32)
+    for g in groups:
+        for n in places(g):
+            back(n).wait_recv()
+        block = returned[g * PER_GROUP : (g + 1) * PER_GROUP].reshape(ROWS, 512)
+        rows = rows + dot(take[:, g * ROWS : (g + 1) * ROWS], block)
+    encoded = third_buf[...].astype(F32) + layer_norm(rows, gain_e_ref[...])
+    for w in range(4):
+        mid = encoded[w * CELLS : (w + 1) * CELLS].reshape(WIN, WIN, 512)
+        edge = encoded[256 + w * CELLS : 256 + (w + 1) * CELLS].reshape(WIN, WIN, 512)
+        w0 = turn(jnp.where(low_cell, mid, edge))
+        w1 = turn(jnp.where(low_cell, edge, mid))
+        block = jnp.concatenate([w0, w1], axis=1).astype(BF16)
+        for half in range(2):
+            top = (w * 8 + 4 + half * 4) % 32
+            enc_ref[0, top : top + 4] = block[half * 4 : half * 4 + 4]
+    for g in groups:
+        for n in places(g):
+            go(n).wait_send()
+            back(n).wait_send()
+
+
+def block_pair(features, routes, tables, gains, weights, shards):
     vmem = pl.BlockSpec(memory_space=pltpu.VMEM)
     hbm = pl.BlockSpec(memory_space=pl.ANY)
     dma = pltpu.SemaphoreType.DMA
     return pl.pallas_call(
-        front_kernel,
-        out_shape=jax.ShapeDtypeStruct((512, 512), BF16),
-        in_specs=[vmem] * 3 + [hbm] * 6,
+        kernel,
+        out_shape=jax.ShapeDtypeStruct((1, 32, 16, 512), BF16),
+        in_specs=[vmem] * 8 + [hbm] * 8,
         out_specs=vmem,
         scratch_shapes=[pltpu.VMEM(w.shape, BF16) for w in weights]
         + [
-            dma((6,)),
+            dma((8,)),
+            pltpu.VMEM((16, 256), F32),
             pltpu.VMEM((4, CELLS, 256), F32),
             pltpu.VMEM((4, CELLS, 256), F32),
             pltpu.VMEM((32, 4, WIN, 512), F32),
             pltpu.VMEM((256, 1536), BF16),
             pltpu.VMEM((256, 1024), BF16),
             pltpu.VMEM((256, 512), BF16),
+            pltpu.VMEM((512, 512), BF16),
         ]
         + [pltpu.VMEM((2, 64, 512), BF16)] * 4
-        + [dma((2, 2)), dma((2, 2))],
+        + [dma((2, 2)), dma((2, 2)), dma((8,)), dma((8,))]
+        + [
+            pltpu.VMEM((4, 512, 512), BF16),
+            pltpu.VMEM((4, 512, 512), BF16),
+            pltpu.VMEM((PEERS * CAP, 512), BF16),
+            pltpu.VMEM((512, PEERS * CAP), BF16),
+        ]
+        + [pltpu.VMEM((PEERS, CAP, 512), BF16)] * 4
+        + [dma((PEERS,))] * 4,
         compiler_params=pltpu.CompilerParams(
-            collective_id=0, has_side_effects=True, vmem_limit_bytes=60 * 1024 * 1024
+            collective_id=0, has_side_effects=True, vmem_limit_bytes=62 * 1024 * 1024
         ),
-        name="front",
-    )(features, flat, gains, *weights)
-
-
-def flat_tables(table):
-    span = 2 * WIN - 1
-    grid = table.reshape(span, span, -1) * LOG2E
-    grid = jnp.pad(grid, ((0, 1), (0, 1), (0, 0)))
-    return grid.reshape(256, -1).T
-
-
-def slot_ids(route_row, experts, capacity):
-    count = route_row.shape[0]
-    onehot = (route_row[:, None] == jnp.arange(experts, dtype=jnp.int32)[None, :]).astype(
-        jnp.bfloat16
-    )
-    order = jnp.arange(count, dtype=jnp.int32)
-    earlier = (order[None, :] < order[:, None]).astype(jnp.bfloat16)
-    ahead = jnp.dot(earlier, onehot, preferred_element_type=jnp.float32)
-    position = jnp.sum(ahead * onehot, axis=-1).astype(jnp.int32)
-    return route_row * capacity + position
-
-
-def regroup(grid):
-    rolled = jnp.roll(grid, (-HALF, -HALF), (0, 1))
-    parts = rolled.reshape((4, WIN, 2, WIN) + grid.shape[2:])
-    return jnp.moveaxis(parts, 2, 0).reshape((-1,) + grid.shape[2:])
-
-
-def ungroup(tokens):
-    parts = tokens.reshape((2, 4, WIN, WIN) + tokens.shape[1:])
-    grid = jnp.moveaxis(parts, 0, 2).reshape((32, 16) + tokens.shape[1:])
-    return jnp.roll(grid, (HALF, HALF), (0, 1))
+        name="block_pair",
+    )(features, routes, *tables, *gains, *weights, *shards)
 
 
 def local(
@@ -372,51 +552,15 @@
     expert_out,
     gain_expert,
 ):
-    weight_in = lax.all_gather(expert_in[0], "band", axis=1, tiled=True)
-    weight_out = lax.all_gather(expert_out[0], "band", axis=0, tiled=True)
-    flat = jnp.concatenate([flat_tables(table_regular), flat_tables(table_shifted)], axis=0)
-    gains = jnp.stack([gain_regular, gain_mlp, gain_shifted, gain_expert])
-    third_out = front(
+    gains = (gain_regular, gain_mlp, gain_shifted, gain_expert)
+    return block_pair(
         features,
-        flat,
-        gains,
+        routes.reshape(32, 16).T.reshape(16, 1, 32),
+        (table_regular.T, table_shifted.T),
+        [g.reshape(1, 512) for g in gains],
         (qkv_regular, proj_regular, mlp_up, mlp_down, qkv_shifted, proj_shifted),
+        (expert_in, expert_out),
     )
-    model_width = 512
-    experts = lax.axis_size("expert")
-    capacity = 32
-    route_rows = regroup(routes.reshape(32, 16))
-    slots = slot_ids(route_rows, experts, capacity)
-    place = (slots[None, :] == jnp.arange(experts * capacity, dtype=jnp.int32)[:, None]).astype(
-        jnp.bfloat16
-    )
-    outgoing = jnp.dot(place, third_out, preferred_element_type=jnp.float32).astype(jnp.bfloat16)
-    arrived = lax.all_to_all(
-        outgoing.reshape(experts, capacity, model_width),
-        "expert",
-        split_axis=0,
-        concat_axis=0,
-        tiled=True,
-    ).reshape(experts * capacity, model_width)
-    hidden = jax.nn.gelu(
-        jnp.dot(arrived, weight_in, preferred_element_type=jnp.float32), approximate=False
-    ).astype(jnp.bfloat16)
-    rows_out = jnp.dot(hidden, weight_out, preferred_element_type=jnp.float32).astype(jnp.bfloat16)
-    returned = lax.all_to_all(
-        rows_out.reshape(experts, capacity, model_width),
-        "expert",
-        split_axis=0,
-        concat_axis=0,
-        tiled=True,
-    ).reshape(experts * capacity, model_width)
-    take = (slots[:, None] == jnp.arange(experts * capacity, dtype=jnp.int32)[None, :]).astype(
-        jnp.bfloat16
-    )
-    expert_rows = jnp.dot(take, returned, preferred_element_type=jnp.float32)
-    encoded = (
-        third_out.astype(jnp.float32) + layer_norm(expert_rows.astype(jnp.float32), gain_expert)
-    ).astype(jnp.bfloat16)
-    return ungroup(encoded)[None]
 
 
 def solution(mesh):

time: 135 us -> 69.3 us (0.51)
  blocking collectives: 50.5 us -> 0 us
  Pallas kernels: 25 us -> 67.3 us
  matrix products: 24.8 us -> 0 us
  between operations: 13.6 us -> 0.01 us
  waiting for transfers between devices: 12.9 us -> 0 us
  other arithmetic: 5.81 us -> 0 us
    all_to_all x2 -> x0, blocking collectives: 50.5 us -> none  [the longest x1 25.8 us: local(): lax.all_to_all(outgoing.reshape(experts, capacity, model_width), 'expert'...]
    pallas_call x1, Pallas kernels: 25 us -> 67.3 us  [block_pair(): pl.pallas_call(kernel, out_shape=jax.ShapeDtypeStruct((1, 32, 16, 512), B...]
    dot_general x4 -> x0, matrix products: 24.8 us -> none  [the longest x1 22 us: local(): jnp.dot(hidden, weight_out, preferred_element_type=jnp.float32)]
    all_gather x2 -> x0, waiting for transfers between devices: 11.5 us -> none  [the longest x1 11.5 us: local(): weight_out = lax.all_gather(expert_out[0], 'band', axis=0, tiled=True)]
    concatenate x4 -> x0, other arithmetic: 2.17 us -> none  [the longest x3 1.55 us: regroup(): rolled = jnp.roll(grid, (-HALF, -HALF), (0, 1))]
    unnamed x10 -> x1, local copies, waits for them, and re-layouts: 0.02 us -> 1.87 us
    mul x2 -> x0, other arithmetic: 1.45 us -> none  [flat_tables(): grid = table.reshape(span, span, -1) * LOG2E]
    unnamed x2 -> x0, waiting for transfers between devices: 1.38 us -> none
  transfers between devices with their start and end apart: 2 -> 0, of which waited for: 1 -> 0; matrix products, arithmetic and copies ran while one was open for 6% -> 0% of each run, Pallas kernels for 19% -> 0%
where the time goes in v2:
time: 69.3 us; the launch traced here: 69.2 us
  Pallas kernels  67.3 us (97%)
  local copies, waits for them, and re-layouts  1.87 us (3%)
    pallas_call x1, Pallas kernels, block_pair(): pl.pallas_call(kernel, out_shape=jax.ShapeDtypeStruct((1, 32, 16, 512), B...  67.3 us
    unnamed x1, local copies, waits for them, and re-layouts  1.87 us

profile of v2, /device:TPU:1, one launch (start us, length us, event | category | flops | bytes accessed | tf_op | source)
XLA Modules:
  0.0 69.2 jit_solution(6213489946243425961)
XLA Ops:
  0.0 67.3 %block_pair.1 = bf16[1,32,16,512]{3,2,1,0:T(8,128)(2,1)} custom-call(bf16[1,32,16,512]{3,2,1,0:T(8,128)(2,1)} %x_ref.1, s32[16,1,32]{2,1,0:T(1,128)} %bitcast.13, f32[16,225]{1,0:T(8,128)} %bitcast.11, f32[16,225]{1,0:T(8,128)} %bitcast.12, f32[1,512]{1,0:T(1,128)} %bitcast.14, f32[1,512]{1,0:T(1,128)} %bitcast.15, f32[1,512]{1,0:T(1,128)} %bitcast.16, ...), custom_call_target="tpu_custom_call" | custom-call | tf_op jit(solution)/shard_map/block_pair/pallas_call | solution.py:503
  67.3 1.9 %copy.18 = bf16[1,32,16,512]{3,2,1,0:T(8,128)(2,1)} copy(bf16[1,32,16,512]{3,2,1,0:T(8,128)(2,1)} %block_pair.1) | data formatting | bytes 1048576

commit v3 on v2

--- a/solution.py
+++ b/solution.py
@@ -170,10 +170,13 @@
     arrived,
     result,
     returned,
+    totals,
     go_send,
     go_recv,
     back_send,
     back_recv,
+    heads_sem,
+    ready_sem,
 ):
     band = lax.axis_index("band")
     bands = lax.axis_size("band")
@@ -189,10 +192,24 @@
         ) * 2 + (my_core + n % 2) % 2
 
     barrier = pltpu.get_barrier_semaphore()
-    for n in range(1, PEERS):
-        pl.semaphore_signal(barrier, inc=1, device_id={"expert": peer(n, 1)}, device_id_type=MESH)
+
+    def tell(sem, to):
+        pl.semaphore_signal(sem, inc=1, device_id={"expert": to}, device_id_type=MESH)
+
+    head = my_z * 8
+    is_head = me == head
+    other_heads = [(head + 8 * n) % PEERS for n in (1, 2, 3)]
     for other in (left, right):
         pl.semaphore_signal(barrier, inc=1, device_id={"band": other}, device_id_type=MESH)
+
+    @pl.when(is_head)
+    def _():
+        for other in other_heads:
+            tell(barrier, other)
+
+    @pl.when(jnp.logical_not(is_head))
+    def _():
+        tell(barrier, head)
 
     loads = [
         pltpu.make_async_copy(src, dst, load_sem.at[n])
@@ -223,16 +240,21 @@
         )
 
     def shard(n):
-        to = {"band": left if n % 2 else right}
-        if n < 2:
-            src, dst = own_in.at[0], w_in.at[1 + n]
-        elif n < 6:
-            rows = pl.ds((n // 2 - 1) * 256, 256)
-            src, dst = own_out.at[0, rows], w_out.at[1 + n % 2, rows]
-        elif n == 6:
-            src, dst = w_in.at[1], w_in.at[3]
+        side = n % 2
+        to = {"band": left if side else right}
+        array, first, count = (
+            (0, 0, 512),
+            (1, 0, 128),
+            (1, 128, 384),
+            (0, side * 256, 256),
+            (1, side * 256, 256),
+        )[n // 2]
+        rows = pl.ds(first, count)
+        kept = (w_in, w_out)[array]
+        if n < 6:
+            src, dst = (own_in, own_out)[array].at[0, rows], kept.at[1 + side, rows]
         else:
-            src, dst = w_out.at[2], w_out.at[3]
+            src, dst = kept.at[1 + side, rows], kept.at[3, rows]
         return remote(src, dst, shard_send.at[n], shard_recv.at[n], to)
 
     def go(n):
@@ -242,6 +264,20 @@
     def back(n):
         to = {"expert": peer(n, -1)}
         return remote(result.at[n], returned.at[n], back_send.at[n], back_recv.at[n], to)
+
+
+    @pl.when(is_head)
+    def _():
+        pl.semaphore_wait(barrier, 2 + 7 + 3)
+        for other in other_heads:
+            tell(heads_sem, other)
+
+    @pl.when(jnp.logical_not(is_head))
+    def _():
+        pl.semaphore_wait(barrier, 2)
+
+    for n in range(2):
+        shard(n).start()
 
     routes = token_routes(routes_ref)
     code = (((routes >> 3) - my_z) & 3) * 4 + (((routes >> 1) - my_x) & 3)
@@ -269,9 +305,13 @@
     window_bias(table_r_ref, pad, bias_r)
     window_bias(table_s_ref, pad, bias_s)
 
-    pl.semaphore_wait(barrier, PEERS - 1 + 2)
-    for n in range(2):
-        shard(n).start()
+
+    @pl.when(is_head)
+    def _():
+        pl.semaphore_wait(heads_sem, 3)
+        for n in range(1, 8):
+            tell(ready_sem, head + n)
+
     for load in loads[:4]:
         load.wait()
 
@@ -347,8 +387,10 @@
     lax.fori_loop(0, 2, first_part, 0)
     for n in (4, 5):
         shard(n).start()
-    shard(0).wait_recv()
-    shard(6).start()
+    for n in (0, 1):
+        shard(n).wait_recv()
+    for n in (6, 7):
+        shard(n).start()
 
     def shifted(column):
         pieces = []
@@ -427,6 +469,10 @@
             ).astype(BF16)
     finish(edge, 256)
 
+    @pl.when(jnp.logical_not(is_head))
+    def _():
+        pl.semaphore_wait(ready_sem, 1)
+
     groups = range(GROUPS)[::-1]
 
     def places(g):
@@ -444,11 +490,10 @@
         for n in places(g):
             go(n).start()
 
-    for n in (3, 5):
+    for n in (2, 3, 4, 5):
         shard(n).wait_recv()
-    shard(7).start()
-    for n in (1, 2, 4):
-        shard(n).wait_recv()
+    for n in (8, 9):
+        shard(n).start()
     for load in loads[6:]:
         load.wait()
 
@@ -456,14 +501,14 @@
         hidden = gelu(dot(rows, w_in[n])).astype(BF16)
         return dot(hidden, w_out[n])
 
-    for g in groups:
+    def near_shards(g):
         for n in places(g):
             go(n).wait_recv()
         rows = arrived[g * PER_GROUP : (g + 1) * PER_GROUP].reshape(ROWS, 512)
-        total = layer(rows, 0) + layer(rows, 1) + layer(rows, 2)
-        if g == GROUPS - 1:
-            for n in (6, 7):
-                shard(n).wait_recv()
+        return layer(rows, 0) + layer(rows, 1) + layer(rows, 2)
+
+    def far_shard(g, total):
+        rows = arrived[g * PER_GROUP : (g + 1) * PER_GROUP].reshape(ROWS, 512)
         block = (total + layer(rows, 3)).astype(BF16).reshape(PER_GROUP, CAP, 512)
         if g == 0:
             returned[0] = block[0]
@@ -472,7 +517,15 @@
             result[g * PER_GROUP : (g + 1) * PER_GROUP] = block
         for n in places(g):
             back(n).start()
-    for n in range(8):
+
+    for g in groups[:-1]:
+        totals[g * ROWS : (g + 1) * ROWS] = near_shards(g)
+    for n in (6, 7, 8, 9):
+        shard(n).wait_recv()
+    for g in groups[:-1]:
+        far_shard(g, totals[g * ROWS : (g + 1) * ROWS])
+    far_shard(0, near_shards(0))
+    for n in range(10):
         shard(n).wait_send()
     rows = jnp.zeros((512, 512), F32)
     for g in groups:
@@ -518,7 +571,7 @@
             pltpu.VMEM((512, 512), BF16),
         ]
         + [pltpu.VMEM((2, 64, 512), BF16)] * 4
-        + [dma((2, 2)), dma((2, 2)), dma((8,)), dma((8,))]
+        + [dma((2, 2)), dma((2, 2)), dma((10,)), dma((10,))]
         + [
             pltpu.VMEM((4, 512, 512), BF16),
             pltpu.VMEM((4, 512, 512), BF16),
@@ -526,7 +579,9 @@
             pltpu.VMEM((512, PEERS * CAP), BF16),
         ]
         + [pltpu.VMEM((PEERS, CAP, 512), BF16)] * 4
-        + [dma((PEERS,))] * 4,
+        + [pltpu.VMEM((PEERS * CAP, 512), F32)]
+        + [dma((PEERS,))] * 4
+        + [pltpu.SemaphoreType.REGULAR] * 2,
         compiler_params=pltpu.CompilerParams(
             collective_id=0, has_side_effects=True, vmem_limit_bytes=62 * 1024 * 1024
         ),

time: 69.3 us -> 66.1 us (0.954)
  Pallas kernels: 67.3 us -> 64.1 us
    pallas_call x1, Pallas kernels: 67.3 us -> 64.1 us  [block_pair(): pl.pallas_call(kernel, out_shape=jax.ShapeDtypeStruct((1, 32, 16, 512), B...]
where the time goes in v3:
time: 66.1 us; the launch traced here: 65.9 us
  Pallas kernels  64.1 us (97%)
  local copies, waits for them, and re-layouts  1.87 us (3%)
    pallas_call x1, Pallas kernels, block_pair(): pl.pallas_call(kernel, out_shape=jax.ShapeDtypeStruct((1, 32, 16, 512), B...  64.1 us
    unnamed x1, local copies, waits for them, and re-layouts  1.87 us

profile of v3, /device:TPU:1, one launch (start us, length us, event | category | flops | bytes accessed | tf_op | source)
XLA Modules:
  0.0 65.9 jit_solution(6538103796861554993)
XLA Ops:
  0.0 64.1 %block_pair.1 = bf16[1,32,16,512]{3,2,1,0:T(8,128)(2,1)} custom-call(bf16[1,32,16,512]{3,2,1,0:T(8,128)(2,1)} %x_ref.1, s32[16,1,32]{2,1,0:T(1,128)} %bitcast.13, f32[16,225]{1,0:T(8,128)} %bitcast.11, f32[16,225]{1,0:T(8,128)} %bitcast.12, f32[1,512]{1,0:T(1,128)} %bitcast.14, f32[1,512]{1,0:T(1,128)} %bitcast.15, f32[1,512]{1,0:T(1,128)} %bitcast.16, ...), custom_call_target="tpu_custom_call" | custom-call | tf_op jit(solution)/shard_map/block_pair/pallas_call | solution.py:556
  64.1 1.9 %copy.18 = bf16[1,32,16,512]{3,2,1,0:T(8,128)(2,1)} copy(bf16[1,32,16,512]{3,2,1,0:T(8,128)(2,1)} %block_pair.1) | data formatting | bytes 1048576

commit v4 on v2

--- a/solution.py
+++ b/solution.py
@@ -174,6 +174,8 @@
     go_recv,
     back_send,
     back_recv,
+    heads_sem,
+    ready_sem,
 ):
     band = lax.axis_index("band")
     bands = lax.axis_size("band")
@@ -181,18 +183,40 @@
     left = lax.rem(band + bands - 1, bands)
     me = lax.axis_index("expert")
     my_z, my_x, my_core = me // 8, (me // 2) % 4, me % 2
-
-    def peer(n, sign):
+    hosted = band // 2
+    mirror = bands - 1 - band
+    beside = hosted * 4 + 1 - band
+    served = jnp.where(my_core == 0, band, mirror)
+    keeper = my_core == hosted
+    sibling = me + 1 - 2 * my_core
+
+    def chip(n, sign):
         z, x = AWAY[n // 2]
-        return (
-            (my_z + 4 + sign * z) % 4 * 4 + (my_x + 4 + sign * x) % 4
-        ) * 2 + (my_core + n % 2) % 2
+        return ((my_z + 4 + sign * z) % 4 * 4 + (my_x + 4 + sign * x) % 4) * 2
 
     barrier = pltpu.get_barrier_semaphore()
-    for n in range(1, PEERS):
-        pl.semaphore_signal(barrier, inc=1, device_id={"expert": peer(n, 1)}, device_id_type=MESH)
-    for other in (left, right):
-        pl.semaphore_signal(barrier, inc=1, device_id={"band": other}, device_id_type=MESH)
+
+    def tell(sem, expert, level):
+        to = {"band": level, "expert": expert}
+        pl.semaphore_signal(sem, inc=1, device_id=to, device_id_type=MESH)
+
+    head = my_z * 8
+    is_head = me == head
+    other_heads = [
+        ((head + 8 * n) % PEERS, level) for level in (band, mirror) for n in range(4)
+    ][1:]
+    tell(barrier, me, left)
+    tell(barrier, me, right)
+    tell(barrier, sibling, band)
+
+    @pl.when(is_head)
+    def _():
+        for other in other_heads:
+            tell(barrier, *other)
+
+    @pl.when(jnp.logical_not(is_head))
+    def _():
+        tell(barrier, head, band)
 
     loads = [
         pltpu.make_async_copy(src, dst, load_sem.at[n])
@@ -209,7 +233,7 @@
             )
         )
     ]
-    for load in loads:
+    for load in loads[:6]:
         load.start()
 
     def remote(src, dst, send_sem, recv_sem, to):
@@ -222,33 +246,79 @@
             device_id_type=MESH,
         )
 
-    def shard(n):
-        to = {"band": left if n % 2 else right}
-        if n < 2:
-            src, dst = own_in.at[0], w_in.at[1 + n]
-        elif n < 6:
-            rows = pl.ds((n // 2 - 1) * 256, 256)
-            src, dst = own_out.at[0, rows], w_out.at[1 + n % 2, rows]
-        elif n == 6:
-            src, dst = w_in.at[1], w_in.at[3]
-        else:
-            src, dst = w_out.at[2], w_out.at[3]
-        return remote(src, dst, shard_send.at[n], shard_recv.at[n], to)
+    shelves = (w_in, w_out)
+    own = (own_in.at[0], own_out.at[0])
+
+    def shard(src, slot, array, n, expert, level):
+        return remote(
+            src,
+            shelves[array].at[slot],
+            shard_send.at[n],
+            shard_recv.at[slot * 2 + array],
+            {"band": level, "expert": expert},
+        )
+
+    def leave(array):
+        slot = jnp.where(keeper, 2, 1)
+        return shard(own[array], slot, array, array, me, jnp.where(keeper, beside, mirror))
+
+    def forward(array):
+        return shard(shelves[array].at[1], 3, array, 2 + array, me, beside)
+
+    def share(slot, array):
+        src = own[array] if slot == 0 else shelves[array].at[slot]
+        return shard(src, slot, array, 4 + slot * 2 + array, sibling, band)
+
+    def came(slot, array):
+        share(slot, array).wait_recv()
 
     def go(n):
-        to = {"expert": peer(n, 1)}
-        return remote(outgoing.at[n], arrived.at[n], go_send.at[n], go_recv.at[n], to)
+        to = {"band": mirror if n % 2 else band, "expert": chip(n, 1) + n % 2}
+        slot = n // 2 * 2 + my_core
+        return remote(outgoing.at[n], arrived.at[slot], go_send.at[n], go_recv.at[slot], to)
 
     def back(n):
-        to = {"expert": peer(n, -1)}
-        return remote(result.at[n], returned.at[n], back_send.at[n], back_recv.at[n], to)
+        to = {"band": served, "expert": chip(n, -1) + n % 2}
+        slot = n // 2 * 2 + my_core
+        return remote(result.at[n], returned.at[slot], back_send.at[n], back_recv.at[slot], to)
+
+    def landed(buffer, sem, n):
+        to = {"band": band, "expert": sibling}
+        remote(buffer.at[n], buffer.at[n], shard_send.at[0], sem.at[n], to).wait_recv()
+
+    def each(places, act):
+        for n in places:
+            if n:
+                act(n)
+            else:
+                pl.when(my_core == 1)(functools.partial(act, n))
+
+    @pl.when(is_head)
+    def _():
+        pl.semaphore_wait(barrier, 3 + 7 + 7)
+        for other in other_heads:
+            tell(heads_sem, *other)
+
+    @pl.when(jnp.logical_not(is_head))
+    def _():
+        pl.semaphore_wait(barrier, 3)
+
+    for array in range(2):
+        leave(array).start()
+
+    @pl.when(keeper)
+    def _():
+        for array in range(2):
+            share(0, array).start()
+        for load in loads[6:]:
+            load.start()
 
     routes = token_routes(routes_ref)
     code = (((routes >> 3) - my_z) & 3) * 4 + (((routes >> 1) - my_x) & 3)
     spot = jnp.zeros_like(routes)
     for n, (z, x) in enumerate(AWAY):
         spot = jnp.where(code == z * 4 + x, n, spot)
-    spot = spot * 2 + ((routes - my_core) & 1)
+    spot = spot * 2 + ((routes - hosted) & 1)
     chosen = lax.broadcasted_iota(jnp.int32, (PEERS, 512), 0) == spot
     onehot = jnp.where(chosen, 1.0, 0.0)
     before = lax.broadcasted_iota(jnp.int32, (512, 512), 0) < lax.broadcasted_iota(
@@ -269,9 +339,13 @@
     window_bias(table_r_ref, pad, bias_r)
     window_bias(table_s_ref, pad, bias_s)
 
-    pl.semaphore_wait(barrier, PEERS - 1 + 2)
-    for n in range(2):
-        shard(n).start()
+
+    @pl.when(is_head)
+    def _():
+        pl.semaphore_wait(heads_sem, 7)
+        for n in range(1, 8):
+            tell(ready_sem, head + n, band)
+
     for load in loads[:4]:
         load.wait()
 
@@ -337,18 +411,24 @@
         for send in sends(part):
             send.start()
 
-        @pl.when(part == 0)
+        @pl.when((part == 0) & keeper)
         def _():
-            for n in (2, 3):
-                shard(n).start()
+            came(1, 0)
+            forward(0).start()
+            share(1, 0).start()
 
         return carry
 
     lax.fori_loop(0, 2, first_part, 0)
-    for n in (4, 5):
-        shard(n).start()
-    shard(0).wait_recv()
-    shard(6).start()
+
+    @pl.when(keeper)
+    def _():
+        came(1, 1)
+        forward(1).start()
+        share(1, 1).start()
+        for array in range(2):
+            came(2, array)
+            share(2, array).start()
 
     def shifted(column):
         pieces = []
@@ -427,57 +507,77 @@
             ).astype(BF16)
     finish(edge, 256)
 
+    @pl.when(jnp.logical_not(is_head))
+    def _():
+        pl.semaphore_wait(ready_sem, 1)
+
     groups = range(GROUPS)[::-1]
 
     def places(g):
-        return range(max(g * PER_GROUP, 1), (g + 1) * PER_GROUP)[::-1]
+        return range(g * PER_GROUP, (g + 1) * PER_GROUP)[::-1]
+
+    def keep(block, buffer):
+        @pl.when(my_core == 0)
+        def _():
+            buffer[0] = block
 
     third = third_buf[...]
     for g in groups:
         block = dot(place[g * ROWS : (g + 1) * ROWS], third).astype(BF16)
         block = block.reshape(PER_GROUP, CAP, 512)
+        outgoing[g * PER_GROUP : (g + 1) * PER_GROUP] = block
         if g == 0:
-            arrived[0] = block[0]
-            outgoing[1:PER_GROUP] = block[1:]
-        else:
-            outgoing[g * PER_GROUP : (g + 1) * PER_GROUP] = block
-        for n in places(g):
-            go(n).start()
-
-    for n in (3, 5):
-        shard(n).wait_recv()
-    shard(7).start()
-    for n in (1, 2, 4):
-        shard(n).wait_recv()
-    for load in loads[6:]:
-        load.wait()
+            keep(block[0], arrived)
+        each(places(g), lambda n: go(n).start())
+
+    @pl.when(keeper)
+    def _():
+        came(3, 0)
+        share(3, 0).start()
+        for load in loads[6:]:
+            load.wait()
+
+    @pl.when(jnp.logical_not(keeper))
+    def _():
+        for slot in range(3):
+            for array in range(2):
+                came(slot, array)
+        came(3, 0)
 
     def layer(rows, n):
         hidden = gelu(dot(rows, w_in[n])).astype(BF16)
         return dot(hidden, w_out[n])
 
     for g in groups:
-        for n in places(g):
-            go(n).wait_recv()
+        each(places(g), lambda n: landed(arrived, go_recv, n))
         rows = arrived[g * PER_GROUP : (g + 1) * PER_GROUP].reshape(ROWS, 512)
         total = layer(rows, 0) + layer(rows, 1) + layer(rows, 2)
         if g == GROUPS - 1:
-            for n in (6, 7):
-                shard(n).wait_recv()
+            came(3, 1)
+
+            @pl.when(keeper)
+            def _():
+                share(3, 1).start()
+
         block = (total + layer(rows, 3)).astype(BF16).reshape(PER_GROUP, CAP, 512)
+        result[g * PER_GROUP : (g + 1) * PER_GROUP] = block
         if g == 0:
-            returned[0] = block[0]
-            result[1:PER_GROUP] = block[1:]
-        else:
-            result[g * PER_GROUP : (g + 1) * PER_GROUP] = block
-        for n in places(g):
-            back(n).start()
-    for n in range(8):
-        shard(n).wait_send()
+            keep(block[0], returned)
+        each(places(g), lambda n: back(n).start())
+
+    for array in range(2):
+        leave(array).wait_send()
+
+    @pl.when(keeper)
+    def _():
+        for array in range(2):
+            forward(array).wait_send()
+            for slot in range(4):
+                share(slot, array).wait_send()
+
     rows = jnp.zeros((512, 512), F32)
     for g in groups:
-        for n in places(g):
-            back(n).wait_recv()
+        each(places(g), lambda n: landed(returned, back_recv, n))
         block = returned[g * PER_GROUP : (g + 1) * PER_GROUP].reshape(ROWS, 512)
         rows = rows + dot(take[:, g * ROWS : (g + 1) * ROWS], block)
     encoded = third_buf[...].astype(F32) + layer_norm(rows, gain_e_ref[...])
@@ -491,9 +591,8 @@
             top = (w * 8 + 4 + half * 4) % 32
             enc_ref[0, top : top + 4] = block[half * 4 : half * 4 + 4]
     for g in groups:
-        for n in places(g):
-            go(n).wait_send()
-            back(n).wait_send()
+        each(places(g), lambda n: go(n).wait_send())
+        each(places(g), lambda n: back(n).wait_send())
 
 
 def block_pair(features, routes, tables, gains, weights, shards):
@@ -518,7 +617,7 @@
             pltpu.VMEM((512, 512), BF16),
         ]
         + [pltpu.VMEM((2, 64, 512), BF16)] * 4
-        + [dma((2, 2)), dma((2, 2)), dma((8,)), dma((8,))]
+        + [dma((2, 2)), dma((2, 2)), dma((12,)), dma((8,))]
         + [
             pltpu.VMEM((4, 512, 512), BF16),
             pltpu.VMEM((4, 512, 512), BF16),
@@ -526,7 +625,8 @@
             pltpu.VMEM((512, PEERS * CAP), BF16),
         ]
         + [pltpu.VMEM((PEERS, CAP, 512), BF16)] * 4
-        + [dma((PEERS,))] * 4,
+        + [dma((PEERS,))] * 4
+        + [pltpu.SemaphoreType.REGULAR] * 2,
         compiler_params=pltpu.CompilerParams(
             collective_id=0, has_side_effects=True, vmem_limit_bytes=62 * 1024 * 1024
         ),

time: 69.3 us -> 66.6 us (0.961)
  the two profiles are of different devices: /device:TPU:1 before, /device:TPU:16 now
where the time goes in v4:
time: 66.6 us; the launch traced here: 66.5 us
  Pallas kernels  64.6 us (97%)
  local copies, waits for them, and re-layouts  1.87 us (3%)
    pallas_call x1, Pallas kernels, block_pair(): pl.pallas_call(kernel, out_shape=jax.ShapeDtypeStruct((1, 32, 16, 512), B...  64.6 us
    unnamed x1, local copies, waits for them, and re-layouts  1.87 us

profile of v4, /device:TPU:16, one launch (start us, length us, event | category | flops | bytes accessed | tf_op | source)
XLA Modules:
  0.0 66.5 jit_solution(15655691053052485839)
XLA Ops:
  0.0 64.6 %block_pair.1 = bf16[1,32,16,512]{3,2,1,0:T(8,128)(2,1)} custom-call(bf16[1,32,16,512]{3,2,1,0:T(8,128)(2,1)} %x_ref.1, s32[16,1,32]{2,1,0:T(1,128)} %bitcast.13, f32[16,225]{1,0:T(8,128)} %bitcast.11, f32[16,225]{1,0:T(8,128)} %bitcast.12, f32[1,512]{1,0:T(1,128)} %bitcast.14, f32[1,512]{1,0:T(1,128)} %bitcast.15, f32[1,512]{1,0:T(1,128)} %bitcast.16, ...), custom_call_target="tpu_custom_call" | custom-call | tf_op jit(solution)/shard_map/block_pair/pallas_call | solution.py:602
  64.6 1.9 %copy.18 = bf16[1,32,16,512]{3,2,1,0:T(8,128)(2,1)} copy(bf16[1,32,16,512]{3,2,1,0:T(8,128)(2,1)} %block_pair.1) | data formatting | bytes 1048576

commit v5 on v4

--- a/solution.py
+++ b/solution.py
@@ -293,26 +293,6 @@
             else:
                 pl.when(my_core == 1)(functools.partial(act, n))
 
-    @pl.when(is_head)
-    def _():
-        pl.semaphore_wait(barrier, 3 + 7 + 7)
-        for other in other_heads:
-            tell(heads_sem, *other)
-
-    @pl.when(jnp.logical_not(is_head))
-    def _():
-        pl.semaphore_wait(barrier, 3)
-
-    for array in range(2):
-        leave(array).start()
-
-    @pl.when(keeper)
-    def _():
-        for array in range(2):
-            share(0, array).start()
-        for load in loads[6:]:
-            load.start()
-
     routes = token_routes(routes_ref)
     code = (((routes >> 3) - my_z) & 3) * 4 + (((routes >> 1) - my_x) & 3)
     spot = jnp.zeros_like(routes)
@@ -329,12 +309,27 @@
     for g in range(GROUPS):
         rows = (lax.broadcasted_iota(jnp.int32, (ROWS, 512), 0) + g * ROWS).astype(F32)
         place[g * ROWS : (g + 1) * ROWS] = jnp.where(rows == slot, 1.0, 0.0).astype(BF16)
-    slot_column = jnp.transpose(jnp.broadcast_to(slot, (LANES, 512)))
-    lane = lax.broadcasted_iota(jnp.int32, (512, LANES), 1).astype(F32)
-    for n in range(PEERS * CAP // LANES):
-        take[:, n * LANES : (n + 1) * LANES] = jnp.where(
-            slot_column == lane + n * LANES, 1.0, 0.0
-        ).astype(BF16)
+
+    @pl.when(is_head)
+    def _():
+        pl.semaphore_wait(barrier, 3 + 7 + 7)
+        for other in other_heads:
+            tell(heads_sem, *other)
+
+    @pl.when(jnp.logical_not(is_head))
+    def _():
+        pl.semaphore_wait(barrier, 3)
+
+    for array in range(2):
+        leave(array).start()
+
+    @pl.when(keeper)
+    def _():
+        for array in range(2):
+            share(0, array).start()
+        for load in loads[6:]:
+            load.start()
+
     scale = LOG2E * 32**-0.5
     window_bias(table_r_ref, pad, bias_r)
     window_bias(table_s_ref, pad, bias_s)
@@ -499,12 +494,12 @@
             v2 = edge_buf[rows, 512 + g * 128 : 640 + g * 128]
             s = jnp.where(low_j, dot_over(k2, q, 1, 1), dot_over(k0, q, 1, 1))
             s = s * scale + bias_s[g] + (mask_both if w == 3 else mask_col)
-            p = soften(s).astype(F32)
-            p = jnp.concatenate([jnp.where(low_j, p, 0.0), jnp.where(low_j, 0.0, p)], axis=0)
-            v = jnp.concatenate([v2, v0], axis=0)
-            heads[rows, g * 128 : g * 128 + 128] = gather_heads(
-                dot_over(p.astype(BF16), v, 0, 0)
-            ).astype(BF16)
+            o = dot_over(soften(s), jnp.concatenate([v2, v0], axis=1), 0, 0)
+            o2 = gather_heads(o[:, :LANES]).reshape(WIN, WIN, LANES)
+            o0 = gather_heads(o[:, LANES:]).reshape(WIN, WIN, LANES)
+            heads[rows, g * 128 : g * 128 + 128] = (
+                jnp.where(cell_is_low((1, WIN, LANES)), o2, o0).reshape(CELLS, LANES).astype(BF16)
+            )
     finish(edge, 256)
 
     @pl.when(jnp.logical_not(is_head))
@@ -529,6 +524,13 @@
         if g == 0:
             keep(block[0], arrived)
         each(places(g), lambda n: go(n).start())
+
+    slot_column = jnp.transpose(jnp.broadcast_to(slot, (LANES, 512)))
+    lane = lax.broadcasted_iota(jnp.int32, (512, LANES), 1).astype(F32)
+    for n in range(PEERS * CAP // LANES):
+        take[:, n * LANES : (n + 1) * LANES] = jnp.where(
+            slot_column == lane + n * LANES, 1.0, 0.0
+        ).astype(BF16)
 
     @pl.when(keeper)
     def _():

time: 66.6 us -> 64 us (0.961)
  Pallas kernels: 64.6 us -> 61.9 us
    pallas_call x1, Pallas kernels: 64.6 us -> 61.9 us  [block_pair(): pl.pallas_call(kernel, out_shape=jax.ShapeDtypeStruct((1, 32, 16, 512), B...]
where the time goes in v5:
time: 64 us; the launch traced here: 63.8 us
  Pallas kernels  61.9 us (97%)
  local copies, waits for them, and re-layouts  1.87 us (3%)
    pallas_call x1, Pallas kernels, block_pair(): pl.pallas_call(kernel, out_shape=jax.ShapeDtypeStruct((1, 32, 16, 512), B...  61.9 us
    unnamed x1, local copies, waits for them, and re-layouts  1.87 us

profile of v5, /device:TPU:16, one launch (start us, length us, event | category | flops | bytes accessed | tf_op | source)
XLA Modules:
  0.0 63.8 jit_solution(6490626413200770136)
XLA Ops:
  0.0 61.9 %block_pair.1 = bf16[1,32,16,512]{3,2,1,0:T(8,128)(2,1)} custom-call(bf16[1,32,16,512]{3,2,1,0:T(8,128)(2,1)} %x_ref.1, s32[16,1,32]{2,1,0:T(1,128)} %bitcast.13, f32[16,225]{1,0:T(8,128)} %bitcast.11, f32[16,225]{1,0:T(8,128)} %bitcast.12, f32[1,512]{1,0:T(1,128)} %bitcast.14, f32[1,512]{1,0:T(1,128)} %bitcast.15, f32[1,512]{1,0:T(1,128)} %bitcast.16, ...), custom_call_target="tpu_custom_call" | custom-call | tf_op jit(solution)/shard_map/block_pair/pallas_call | solution.py:604
  61.9 1.9 %copy.18 = bf16[1,32,16,512]{3,2,1,0:T(8,128)(2,1)} copy(bf16[1,32,16,512]{3,2,1,0:T(8,128)(2,1)} %block_pair.1) | data formatting | bytes 1048576

commit v6 on v5

--- a/solution.py
+++ b/solution.py
@@ -406,21 +406,16 @@
         for send in sends(part):
             send.start()
 
-        @pl.when((part == 0) & keeper)
-        def _():
-            came(1, 0)
-            forward(0).start()
-            share(1, 0).start()
-
         return carry
 
     lax.fori_loop(0, 2, first_part, 0)
 
     @pl.when(keeper)
     def _():
-        came(1, 1)
-        forward(1).start()
-        share(1, 1).start()
+        for array in range(2):
+            came(1, array)
+            forward(array).start()
+            share(1, array).start()
         for array in range(2):
             came(2, array)
             share(2, array).start()

time: 64 us -> 61.3 us (0.958)
  the two profiles are of different devices: /device:TPU:16 before, /device:TPU:1 now
where the time goes in v6:
time: 61.3 us; the launch traced here: 61.1 us
  Pallas kernels  59.2 us (97%)
  local copies, waits for them, and re-layouts  1.87 us (3%)
    pallas_call x1, Pallas kernels, block_pair(): pl.pallas_call(kernel, out_shape=jax.ShapeDtypeStruct((1, 32, 16, 512), B...  59.2 us
    unnamed x1, local copies, waits for them, and re-layouts  1.87 us

profile of v6, /device:TPU:1, one launch (start us, length us, event | category | flops | bytes accessed | tf_op | source)
XLA Modules:
  0.0 61.1 jit_solution(1712686946139886193)
XLA Ops:
  0.0 59.2 %block_pair.1 = bf16[1,32,16,512]{3,2,1,0:T(8,128)(2,1)} custom-call(bf16[1,32,16,512]{3,2,1,0:T(8,128)(2,1)} %x_ref.1, s32[16,1,32]{2,1,0:T(1,128)} %bitcast.13, f32[16,225]{1,0:T(8,128)} %bitcast.11, f32[16,225]{1,0:T(8,128)} %bitcast.12, f32[1,512]{1,0:T(1,128)} %bitcast.14, f32[1,512]{1,0:T(1,128)} %bitcast.15, f32[1,512]{1,0:T(1,128)} %bitcast.16, ...), custom_call_target="tpu_custom_call" | custom-call | tf_op jit(solution)/shard_map/block_pair/pallas_call | solution.py:599
  59.2 1.9 %copy.18 = bf16[1,32,16,512]{3,2,1,0:T(8,128)(2,1)} copy(bf16[1,32,16,512]{3,2,1,0:T(8,128)(2,1)} %block_pair.1) | data formatting | bytes 1048576

commit v7 on v6

--- a/solution.py
+++ b/solution.py
@@ -412,13 +412,9 @@
 
     @pl.when(keeper)
     def _():
-        for array in range(2):
-            came(1, array)
-            forward(array).start()
-            share(1, array).start()
-        for array in range(2):
-            came(2, array)
-            share(2, array).start()
+        came(1, 0)
+        forward(0).start()
+        share(1, 0).start()
 
     def shifted(column):
         pieces = []
@@ -461,6 +457,15 @@
                 dot_over(soften(s), v, 0, 0)
             ).astype(BF16)
     finish(mid, 0)
+
+    @pl.when(keeper)
+    def _():
+        came(1, 1)
+        forward(1).start()
+        share(1, 1).start()
+        for array in range(2):
+            came(2, array)
+            share(2, array).start()
 
     for part in range(2):
         for send in sends(part):
@@ -501,7 +506,7 @@
     def _():
         pl.semaphore_wait(ready_sem, 1)
 
-    groups = range(GROUPS)[::-1]
+    groups = range(GROUPS)
 
     def places(g):
         return range(g * PER_GROUP, (g + 1) * PER_GROUP)[::-1]
@@ -549,7 +554,7 @@
         each(places(g), lambda n: landed(arrived, go_recv, n))
         rows = arrived[g * PER_GROUP : (g + 1) * PER_GROUP].reshape(ROWS, 512)
         total = layer(rows, 0) + layer(rows, 1) + layer(rows, 2)
-        if g == GROUPS - 1:
+        if g == groups[0]:
             came(3, 1)
 
             @pl.when(keeper)

time: 61.3 us -> 61.9 us (level)
  the two profiles are of different devices: /device:TPU:1 before, /device:TPU:16 now
where the time goes in v7:
time: 61.9 us; the launch traced here: 61.7 us
  Pallas kernels  59.8 us (97%)
  local copies, waits for them, and re-layouts  1.87 us (3%)
    pallas_call x1, Pallas kernels, block_pair(): pl.pallas_call(kernel, out_shape=jax.ShapeDtypeStruct((1, 32, 16, 512), B...  59.8 us
    unnamed x1, local copies, waits for them, and re-layouts  1.87 us

profile of v7, /device:TPU:16, one launch (start us, length us, event | category | flops | bytes accessed | tf_op | source)
XLA Modules:
  0.0 61.7 jit_solution(2319713722357760536)
XLA Ops:
  0.0 59.8 %block_pair.1 = bf16[1,32,16,512]{3,2,1,0:T(8,128)(2,1)} custom-call(bf16[1,32,16,512]{3,2,1,0:T(8,128)(2,1)} %x_ref.1, s32[16,1,32]{2,1,0:T(1,128)} %bitcast.13, f32[16,225]{1,0:T(8,128)} %bitcast.11, f32[16,225]{1,0:T(8,128)} %bitcast.12, f32[1,512]{1,0:T(1,128)} %bitcast.14, f32[1,512]{1,0:T(1,128)} %bitcast.15, f32[1,512]{1,0:T(1,128)} %bitcast.16, ...), custom_call_target="tpu_custom_call" | custom-call | tf_op jit(solution)/shard_map/block_pair/pallas_call | solution.py:604
  59.8 1.9 %copy.18 = bf16[1,32,16,512]{3,2,1,0:T(8,128)(2,1)} copy(bf16[1,32,16,512]{3,2,1,0:T(8,128)(2,1)} %block_pair.1) | data formatting | bytes 1048576

commit v8 on v6

--- a/solution.py
+++ b/solution.py
@@ -310,6 +310,9 @@
         rows = (lax.broadcasted_iota(jnp.int32, (ROWS, 512), 0) + g * ROWS).astype(F32)
         place[g * ROWS : (g + 1) * ROWS] = jnp.where(rows == slot, 1.0, 0.0).astype(BF16)
 
+    window_bias(table_r_ref, pad, bias_r)
+    window_bias(table_s_ref, pad, bias_s)
+
     @pl.when(is_head)
     def _():
         pl.semaphore_wait(barrier, 3 + 7 + 7)
@@ -331,8 +334,6 @@
             load.start()
 
     scale = LOG2E * 32**-0.5
-    window_bias(table_r_ref, pad, bias_r)
-    window_bias(table_s_ref, pad, bias_s)
 
 
     @pl.when(is_head)
@@ -501,7 +502,7 @@
     def _():
         pl.semaphore_wait(ready_sem, 1)
 
-    groups = range(GROUPS)[::-1]
+    groups = range(GROUPS)
 
     def places(g):
         return range(g * PER_GROUP, (g + 1) * PER_GROUP)[::-1]
@@ -549,7 +550,7 @@
         each(places(g), lambda n: landed(arrived, go_recv, n))
         rows = arrived[g * PER_GROUP : (g + 1) * PER_GROUP].reshape(ROWS, 512)
         total = layer(rows, 0) + layer(rows, 1) + layer(rows, 2)
-        if g == GROUPS - 1:
+        if g == groups[0]:
             came(3, 1)
 
             @pl.when(keeper)

time: 61.3 us -> 61.2 us (level); the launches traced: 61.1 us -> 60.4 us
  Pallas kernels: 59.2 us -> 58.5 us
    pallas_call x1, Pallas kernels: 59.2 us -> 58.5 us  [block_pair(): pl.pallas_call(kernel, out_shape=jax.ShapeDtypeStruct((1, 32, 16, 512), B...]
where the time goes in v8:
time: 61.2 us; the launch traced here: 60.4 us
  Pallas kernels  58.5 us (96%)
  local copies, waits for them, and re-layouts  1.87 us (3%)
    pallas_call x1, Pallas kernels, block_pair(): pl.pallas_call(kernel, out_shape=jax.ShapeDtypeStruct((1, 32, 16, 512), B...  58.5 us
    unnamed x1, local copies, waits for them, and re-layouts  1.87 us

profile of v8, /device:TPU:1, one launch (start us, length us, event | category | flops | bytes accessed | tf_op | source)
XLA Modules:
  0.0 60.4 jit_solution(15810453965248039014)
XLA Ops:
  0.0 58.5 %block_pair.1 = bf16[1,32,16,512]{3,2,1,0:T(8,128)(2,1)} custom-call(bf16[1,32,16,512]{3,2,1,0:T(8,128)(2,1)} %x_ref.1, s32[16,1,32]{2,1,0:T(1,128)} %bitcast.13, f32[16,225]{1,0:T(8,128)} %bitcast.11, f32[16,225]{1,0:T(8,128)} %bitcast.12, f32[1,512]{1,0:T(1,128)} %bitcast.14, f32[1,512]{1,0:T(1,128)} %bitcast.15, f32[1,512]{1,0:T(1,128)} %bitcast.16, ...), custom_call_target="tpu_custom_call" | custom-call | tf_op jit(solution)/shard_map/block_pair/pallas_call | solution.py:600
  58.5 1.9 %copy.18 = bf16[1,32,16,512]{3,2,1,0:T(8,128)(2,1)} copy(bf16[1,32,16,512]{3,2,1,0:T(8,128)(2,1)} %block_pair.1) | data formatting | bytes 1048576

commit v9 on v8

--- a/solution.py
+++ b/solution.py
@@ -417,9 +417,6 @@
             came(1, array)
             forward(array).start()
             share(1, array).start()
-        for array in range(2):
-            came(2, array)
-            share(2, array).start()
 
     def shifted(column):
         pieces = []
@@ -462,6 +459,12 @@
                 dot_over(soften(s), v, 0, 0)
             ).astype(BF16)
     finish(mid, 0)
+
+    @pl.when(keeper)
+    def _():
+        for array in range(2):
+            came(2, array)
+            share(2, array).start()
 
     for part in range(2):
         for send in sends(part):

time: 61.2 us -> 61 us (level)
  no operation moved by 1% of the time
where the time goes in v9:
time: 61 us; the launch traced here: 60.4 us
  Pallas kernels  58.5 us (96%)
  local copies, waits for them, and re-layouts  1.87 us (3%)
    pallas_call x1, Pallas kernels, block_pair(): pl.pallas_call(kernel, out_shape=jax.ShapeDtypeStruct((1, 32, 16, 512), B...  58.5 us
    unnamed x1, local copies, waits for them, and re-layouts  1.87 us

profile of v9, /device:TPU:1, one launch (start us, length us, event | category | flops | bytes accessed | tf_op | source)
XLA Modules:
  0.0 60.4 jit_solution(6039722444258319376)
XLA Ops:
  0.0 58.5 %block_pair.1 = bf16[1,32,16,512]{3,2,1,0:T(8,128)(2,1)} custom-call(bf16[1,32,16,512]{3,2,1,0:T(8,128)(2,1)} %x_ref.1, s32[16,1,32]{2,1,0:T(1,128)} %bitcast.13, f32[16,225]{1,0:T(8,128)} %bitcast.11, f32[16,225]{1,0:T(8,128)} %bitcast.12, f32[1,512]{1,0:T(1,128)} %bitcast.14, f32[1,512]{1,0:T(1,128)} %bitcast.15, f32[1,512]{1,0:T(1,128)} %bitcast.16, ...), custom_call_target="tpu_custom_call" | custom-call | tf_op jit(solution)/shard_map/block_pair/pallas_call | solution.py:603
  58.5 1.9 %copy.18 = bf16[1,32,16,512]{3,2,1,0:T(8,128)(2,1)} copy(bf16[1,32,16,512]{3,2,1,0:T(8,128)(2,1)} %block_pair.1) | data formatting | bytes 1048576
